TPU v7x, 128 devices: a whole 4x4x4 slice. The times are simulated.
128 devices in a mesh: grp: 8 (over y, core), nbr: 16 (over x, z).
Axes of the slice: x: 4, y: 4, z: 4, core: 2. Of those that a mesh axis runs over, the one named last changes fastest.
Arguments:
- sims: float32 [2048, 128, 128], P(('grp', 'nbr')), may hold values from -6 to 6
- own_tiles: float32 [24576, 128, 128], P(('grp', 'nbr')), may hold values from -0.15625 to 0.15625
- own_cols: int32 [24576], P(('grp', 'nbr')), may hold values from 0 to 271
- own_rows: int32 [24576], P(('grp', 'nbr')), may hold values from 0 to 15
- help_tiles: float32 [4096, 128, 128], P(('grp', 'nbr')), may hold values from -0.15625 to 0.15625
- help_cols: int32 [4096], P(('grp', 'nbr')), may hold values from 0 to 271
- help_rows: int32 [4096], P(('grp', 'nbr')), may hold values from 0 to 15
- help_live: int32 [4096], P(('grp', 'nbr')), may hold values from 0 to 1, as said below
Outputs:
- reobserved: float32 [2048, 128, 128], P(('grp', 'nbr'))
Inputs may be any that keep to these rules, and one draw needn't show every extreme that they name: `help_live`: helper slot j of a device serves the owner of neighbour index j // 2 in the same group, so at most 2 live slots go from one device to one owner; in every group one owner receives all 2 slots live from every device of the group.
All inputs are finite; a program needn't handle non-finite values.
Results may differ from a plain program's by a relative error of at most 0.0001.
Values sent between devices are 32-bit elements; how exact they have to be, the bound alone decides.
A program may use at most 192 MiB of HBM per device.

v0:
```python
import jax
import jax.numpy as jnp
from jax import lax
from jax.sharding import PartitionSpec as P

RIM = 8


def padded(shard, sides, width):
    for axis, dim in sides:
        peers, length = (lax.axis_size(axis), shard.shape[dim])
        up = [(i, (i + 1) % peers) for i in range(peers - 1)]
        down = [(j, i) for i, j in up]
        last = lax.slice_in_dim(shard, length - width, length, axis=dim)
        initial = lax.slice_in_dim(shard, 0, width, axis=dim)
        before = lax.ppermute(last, axis, up)
        after = lax.ppermute(initial, axis, down)
        shard = jnp.concatenate([before, shard, after], axis=dim)
    return shard


def pick_from(source, first, cols):
    length = source.shape[0]
    index = cols - first
    valid = ((index >= 0) & (index < length)).astype(jnp.float32)
    taken = jnp.take(source, jnp.clip(index, 0, length - 1), axis=0)
    return taken * valid[:, None, None]


def local(sims, own_tiles, own_cols, own_rows, help_tiles, help_cols, help_rows, help_live):
    high = lax.Precision.HIGHEST
    rows_dev = sims.shape[0]
    neighbours = lax.axis_size("nbr")
    group_rows = rows_dev * neighbours
    help_dev = help_tiles.shape[0]
    slots_owner = help_dev // neighbours
    group = lax.all_gather(sims, "nbr", axis=0, tiled=True)
    own_pick = pick_from(group, RIM, own_cols)
    help_pick = pick_from(group, RIM, help_cols)
    edges = jnp.concatenate([group[:RIM], group[group_rows - RIM :]], axis=0)
    rims = padded(edges, (("grp", 0),), RIM)
    lower = rims[:RIM]
    upper = rims[rims.shape[0] - RIM :]
    own_pick = (
        own_pick + pick_from(lower, 0, own_cols) + pick_from(upper, RIM + group_rows, own_cols)
    )
    help_pick = (
        help_pick + pick_from(lower, 0, help_cols) + pick_from(upper, RIM + group_rows, help_cols)
    )
    own_terms = jnp.einsum("tij,tjs->tis", own_tiles, own_pick, precision=high)
    select = (own_rows[None, :] == jnp.arange(rows_dev, dtype=jnp.int32)[:, None]).astype(
        jnp.float32
    )
    own_sum = jnp.einsum("rt,tis->ris", select, own_terms, precision=high)
    help_terms = (
        jnp.einsum("tij,tjs->tis", help_tiles, help_pick, precision=high)
        * help_live.astype(jnp.float32)[:, None, None]
    )
    outgoing = help_terms.reshape(neighbours, slots_owner, help_terms.shape[1], help_terms.shape[2])
    out_rows = help_rows.astype(jnp.float32).reshape(neighbours, slots_owner)
    incoming, in_rows = (
        lax.all_to_all(outgoing, "nbr", split_axis=0, concat_axis=0, tiled=True),
        lax.all_to_all(out_rows, "nbr", split_axis=0, concat_axis=0, tiled=True),
    )
    flat_terms = incoming.reshape(help_dev, incoming.shape[2], incoming.shape[3])
    flat_rows = in_rows.reshape(help_dev)
    picker = (flat_rows[None, :] == jnp.arange(rows_dev, dtype=jnp.float32)[:, None]).astype(
        jnp.float32
    )
    help_sum = jnp.einsum("rt,tis->ris", picker, flat_terms, precision=high)
    return own_sum + help_sum


def solution(mesh):
    placed = (
        P(("grp", "nbr"), None, None),
        P(("grp", "nbr"), None, None),
        P(("grp", "nbr")),
        P(("grp", "nbr")),
        P(("grp", "nbr"), None, None),
        P(("grp", "nbr")),
        P(("grp", "nbr")),
        P(("grp", "nbr")),
    )
    return jax.shard_map(
        local, mesh=mesh, in_specs=placed, out_specs=P(("grp", "nbr"), None, None), check_vma=False
    )
```

profile of v0, /device:TPU:1, one launch (start us, length us, event | category | flops | bytes accessed | tf_op | source)
XLA Modules:
  0.0 253.4 jit_solution(752253415979622065)
XLA Ops:
  6.5 0.0 copy-start
  6.5 0.0 copy-start.2
  6.5 0.0 copy-start.4
  6.5 0.0 all-gather.2.cloned.1.call-start
  6.5 0.7 all-gather.2.cloned.1.call-update
  7.3 0.7 convert_element_type.29
  7.9 0.7 all_to_all.9
  8.6 8.4 %all-to-all-start = ((f32[16,1,2]{2,1,0:T(1,128)}), f32[16,1,2]{2,1,0:T(1,128)S(1)}, u32[]{:S(2)}, u32[]{:S(2)}) async-start(f32[16,1,2]{2,1,0:T(1,128)} %bitcast.2), calls=%async_computation | async-start | bytes 16384 | tf_op jit(solution)/shard_map/all_to_all | solution.py:63
  17.0 0.7 compare_select_fusion.1
  17.7 0.7 and_convert_fusion.2
  18.4 105.5 %all-gather.2.cloned.1.call-done = f32[256,128,128]{2,1,0:T(8,128)} async-done(((f32[16,128,128]{2,1,0:T(8,128)}), f32[256,128,128]{2,1,0:T(8,128)}) %all-gather.2.cloned.1.call-update) | async-done | bytes 16777232 | tf_op jit(solution)/shard_map/all_gather | solution.py:37
  123.9 2.3 fusion.43
  126.1 3.8 %collective-permute-start = (f32[8,128,128]{2,1,0:T(8,128)}, f32[8,128,128]{2,1,0:T(8,128)S(1)}, u32[]{:S(2)}, u32[]{:S(2)}) collective-permute-start(f32[8,128,128]{2,1,0:T(8,128)} %get-tuple-element.17), channel_id=1, source_target_pairs={{0,16},{16,32},{32,48},{48,64},{64,80},{80,96},{96,112},{1,17},{17... | collective-permute-start | bytes 1572872 | tf_op jit(solution)/shard_map/ppermute | solution.py:16
  130.0 1.9 collective-permute-start.1
  131.9 0.0 copy-done.2
  132.0 0.0 copy-done.4
  132.0 0.0 all-to-all-done
  132.0 0.5 broadcast.82
  132.5 0.6 reduce.3
  133.1 0.1 eq.31
  133.2 7.7 %gather_fusion.1 = f32[32,128,128]{2,1,0:T(8,128)} fusion(f32[256,128,128]{2,1,0:T(8,128)} %all-gather.2.cloned.1.call-done, s32[1024]{0:T(1024)S(1)} %pad_clamp_fusion.2), kind=kCustom, calls=%fused_computation.5 | custom fusion | bytes 4194432 | tf_op jit(solution)/shard_map/jit(_take)/gather | solution.py:26
  140.9 16.5 %gather_fusion = f32[192,128,128]{2,1,0:T(8,128)} fusion(f32[256,128,128]{2,1,0:T(8,128)} %all-gather.2.cloned.1.call-done, s32[1024]{0:T(1024)S(1)} %get-tuple-element.37), kind=kCustom, calls=%fused_computation.4 | custom fusion | bytes 25166592 | tf_op jit(solution)/shard_map/jit(_take)/gather | solution.py:26
  157.4 0.0 collective-permute-done.1
  157.4 2.0 gather_fusion.5
  159.4 0.0 collective-permute-done
  159.4 2.0 gather_fusion.4
  161.4 0.0 copy-done
  161.4 8.3 %fusion.24 = f32[32,128,128]{2,1,0:T(8,128)} fusion(f32[32,128,128]{2,1,0:T(8,128)S(1)} %copy-done, f32[32,128,128]{2,1,0:T(8,128)} %gather_fusion.5, f32[32,128,128]{2,1,0:T(8,128)} %gather_fusion.4, f32[32,128,128]{2,1,0:T(8,128)} %gather_fusion.1, f32[32]{0:T(128)S(1)} %convert_element_type.33, f32[32]{0:T(128)S(1)} %get-tuple-element.28, ...), kind=kOutput, calls=%fused_computation.28 | convolution fusion | flops 810024960 | bytes 10486368 | tf_op jit(solution)/shard_map/tij,tjs->tis/dot_general | solution.py:56
  169.7 5.0 %all-to-all-start.1 = ((f32[16,2,128,128]{2,3,1,0:T(8,128)}), f32[16,2,128,128]{2,3,1,0:T(8,128)S(1)}, u32[]{:S(2)}, u32[]{:S(2)}) async-start(f32[16,2,128,128]{2,3,1,0:T(8,128)} %bitcast.18), calls=%async_computation.1 | async-start | bytes 4194304 | tf_op jit(solution)/shard_map/all_to_all | solution.py:62
  174.7 5.9 %gather_fusion.2 = f32[192,128,128]{2,1,0:T(8,128)} fusion(f32[8,128,128]{2,1,0:T(8,128)S(1)} %collective-permute-done, s32[1024]{0:T(1024)S(1)} %pad_clamp_fusion.4), kind=kCustom, calls=%fused_computation.clone | custom fusion | bytes 25166592 | tf_op jit(solution)/shard_map/jit(_take)/gather | solution.py:26
  180.7 5.9 %gather_fusion.3 = f32[192,128,128]{2,1,0:T(8,128)} fusion(f32[8,128,128]{2,1,0:T(8,128)S(1)} %collective-permute-done.1, s32[1024]{0:T(1024)S(1)} %get-tuple-element.36), kind=kCustom, calls=%fused_computation.2.clone | custom fusion | bytes 25166592 | tf_op jit(solution)/shard_map/jit(_take)/gather | solution.py:26
  186.6 33.9 %fusion.14 = f32[192,128,128]{1,2,0:T(8,128)} fusion(f32[192,128,128]{2,1,0:T(8,128)} %param.13, f32[192,128,128]{2,1,0:T(8,128)} %gather_fusion.3, f32[192,128,128]{2,1,0:T(8,128)} %gather_fusion.2, f32[192,128,128]{2,1,0:T(8,128)} %gather_fusion, f32[192]{0:T(256)S(1)} %get-tuple-element.21, f32[192]{0:T(256)S(1)} %get-tuple-element.26, ...), kind=kOutput, calls=%fused_computation.20 | convolution fusion | flops 4857004032 | bytes 62917440 | tf_op jit(solution)/shard_map/tij,tjs->tis/dot_general | solution.py:50
  220.4 0.0 copy-start.3
  220.4 12.7 %copy.16 = f32[192,128,128]{2,0,1:T(8,128)} copy(f32[192,128,128]{1,2,0:T(8,128)} %fusion.14) | data formatting | bytes 25165824 | tf_op jit(solution)/shard_map/tij,tjs->tis/dot_general | solution.py:50
  233.1 0.0 copy-done.3
  233.1 7.1 %fusion.35 = f32[16,128,128]{2,0,1:T(8,128)S(1)} fusion(f32[192,128,128]{2,0,1:T(8,128)} %copy.16, s32[192]{0:T(256)S(1)} %copy-done.3), kind=kOutput, calls=%fused_computation.39 | convolution fusion | flops 603982848 | bytes 13632256 | tf_op jit(solution)/shard_map/rt,tis->ris/dot_general | solution.py:54
  240.2 0.0 all-to-all-done.1
  240.2 2.5 copy.19
  242.7 0.0 copy-start.1
  242.7 2.5 %convolution_add_fusion = f32[16,128,128]{2,0,1:T(8,128)S(1)} fusion(f32[16,128,128]{2,0,1:T(8,128)S(1)} %fusion.35, f32[32,128,128]{2,0,1:T(8,128)} %bitcast.17, f32[32]{0:T(128)S(1)} %eq.31), kind=kOutput, calls=%fused_computation.29 | convolution fusion | flops 100925952 | bytes 4194432 | tf_op jit(solution)/shard_map/rt,tis->ris/dot_general | solution.py:70
  245.2 1.3 copy.20
  246.5 0.0 copy-done.1
  (6 shorter events, 0.0 us)
Async XLA Ops:
  6.5 154.9 %copy-start = (f32[32,128,128]{2,1,0:T(8,128)S(1)}, f32[32,128,128]{2,1,0:T(8,128)}, u32[]{:S(2)}) copy-start(f32[32,128,128]{2,1,0:T(8,128)} %param.16) | copy-start | bytes 6291460
  6.5 125.4 %copy-start.2 = (s32[192]{0:T(256)S(1)}, s32[192]{0:T(256)}, u32[]{:S(2)}) copy-start(s32[192]{0:T(256)} %param.14) | copy-start | bytes 2308
  6.5 125.4 %copy-start.4 = (s32[32]{0:T(128)S(1)}, s32[32]{0:T(128)}, u32[]{:S(2)}) copy-start(s32[32]{0:T(128)} %param.19) | copy-start | bytes 388
  6.5 117.3 %all-gather.2.cloned.1.call-start = ((), (), s32[]{:S(2)}) async-start(), calls=%async_computation.2 | async-start | bytes 17825792 | tf_op jit(solution)/shard_map/all_gather | solution.py:37
  8.6 123.4 %all-to-all-start = ((f32[16,1,2]{2,1,0:T(1,128)}), f32[16,1,2]{2,1,0:T(1,128)S(1)}, u32[]{:S(2)}, u32[]{:S(2)}) async-start(f32[16,1,2]{2,1,0:T(1,128)} %bitcast.2), calls=%async_computation | async-start | bytes 16384 | tf_op jit(solution)/shard_map/all_to_all | solution.py:63
  126.1 33.3 %collective-permute-start = (f32[8,128,128]{2,1,0:T(8,128)}, f32[8,128,128]{2,1,0:T(8,128)S(1)}, u32[]{:S(2)}, u32[]{:S(2)}) collective-permute-start(f32[8,128,128]{2,1,0:T(8,128)} %get-tuple-element.17), channel_id=1, source_target_pairs={{0,16},{16,32},{32,48},{48,64},{64,80},{80,96},{96,112},{1,17},{17... | collective-permute-start | bytes 1572872 | tf_op jit(solution)/shard_map/ppermute | solution.py:16
  130.0 27.4 %collective-permute-start.1 = (f32[8,128,128]{2,1,0:T(8,128)}, f32[8,128,128]{2,1,0:T(8,128)S(1)}, u32[]{:S(2)}, u32[]{:S(2)}) collective-permute-start(f32[8,128,128]{2,1,0:T(8,128)} %get-tuple-element.18), channel_id=1, source_target_pairs={{16,0},{32,16},{48,32},{64,48},{80,64},{96,80},{112,96},{17,1},{33... | collective-permute-start | bytes 1572872 | tf_op jit(solution)/shard_map/ppermute | solution.py:17
  169.7 70.5 %all-to-all-start.1 = ((f32[16,2,128,128]{2,3,1,0:T(8,128)}), f32[16,2,128,128]{2,3,1,0:T(8,128)S(1)}, u32[]{:S(2)}, u32[]{:S(2)}) async-start(f32[16,2,128,128]{2,3,1,0:T(8,128)} %bitcast.18), calls=%async_computation.1 | async-start | bytes 4194304 | tf_op jit(solution)/shard_map/all_to_all | solution.py:62
  220.4 12.7 %copy-start.3 = (s32[192]{0:T(256)S(1)}, s32[192]{0:T(256)}, u32[]{:S(2)}) copy-start(s32[192]{0:T(256)} %param.15) | copy-start | bytes 2308
  242.7 3.8 %copy-start.1 = (f32[32,128,128]{2,1,0:T(8,128)S(1)}, f32[32,128,128]{2,1,0:T(8,128)}, u32[]{:S(2)}) copy-start(f32[32,128,128]{2,1,0:T(8,128)} %param.16) | copy-start | bytes 6291460
Sparse Core Ops, SparseCore 0:
  9.5 114.3 all-gather.1
where the time goes:
time: 254 us; the launch traced here: 253 us
  waiting for transfers between devices  106 us (42%)
  local copies, waits for them, and re-layouts  60.1 us (24%)
  matrix products  51.8 us (20%)
  starting transfers between devices  19.1 us (8%)
  between operations  13.5 us (5%)
  other arithmetic  2.63 us (1%)
    all_gather x1, waiting for transfers between devices, local(): group = lax.all_gather(sims, 'nbr', axis=0, tiled=True)  105 us
    gather x6, local copies, waits for them, and re-layouts, pick_from(): taken = jnp.take(source, jnp.clip(index, 0, length - 1), axis=0)  40.1 us
    dot_general x1, matrix products, local(): own_terms = jnp.einsum('tij,tjs->tis', own_tiles, own_pick, precision=high)  33.9 us
    dot_general x1, local copies, waits for them, and re-layouts, local(): own_terms = jnp.einsum('tij,tjs->tis', own_tiles, own_pick, precision=high)  12.7 us
    all_to_all x1, starting transfers between devices, local(): lax.all_to_all(out_rows, 'nbr', split_axis=0, concat_axis=0, tiled=True)  8.42 us
    dot_general x1, matrix products, local(): jnp.einsum('tij,tjs->tis', help_tiles, help_pick, precision=high)  8.31 us
    dot_general x1, matrix products, local(): own_sum = jnp.einsum('rt,tis->ris', select, own_terms, precision=high)  7.07 us
  transfers between devices with their start and end apart: 5, of which 1 were waited for; matrix products, arithmetic and copies ran while one was open for 38% of the time, Pallas kernels for 0%

commit v1 on v0

v1 whole, which is shorter than its diff:
```python
import functools

import jax
import jax.numpy as jnp
from jax import lax
from jax.experimental import pallas as pl
from jax.experimental.pallas import tpu as pltpu
from jax.sharding import PartitionSpec as P

RIM = 8
UNIT = 4
SIDE = 4
DEPTH = 8
MESH = pl.DeviceIdType.MESH


def unit_id(origin, sub):
    return ((origin[0] % SIDE) * SIDE + origin[1] % SIDE) * 4 + sub


def gather_queues():
    queues = []
    for axis in (0, 1):
        for way in (1, -1):
            near, far = ((0, 1), (2, 3)) if axis == 0 else ((2, 3), (0, 1))
            if way < 0:
                near, far = near[::-1], far[::-1]

            def at(along, across, axis=axis):
                return (along, across) if axis == 0 else (across, along)

            queue = [
                (at(0, 0), near[0]),
                (at(0, 0), near[1]),
                (at(0, 0), far[0]),
                (at(-way, 0), near[0]),
                (at(0, 0), far[1]),
                (at(0, -1), far[0]),
                (at(0, 1), far[0]),
                (at(0, -1), far[1]),
                (at(0, 1), far[1]),
                (at(0, 2), far[0]),
                (at(0, 2), far[1]),
                (at(-way, 0), far[0]),
                (at(-way, -1), far[0]),
                (at(-way, 1), far[0]),
                (at(-way, 2), far[0]),
            ]
            queues.append((axis, way, queue))
    return queues


class Link:
    def __init__(self, send, recv):
        self.send, self.recv, self.sent = send, recv, []

    def start(self, src, dst, arrival, device):
        copy = pltpu.make_async_remote_copy(
            src_ref=src,
            dst_ref=dst,
            send_sem=self.send.at[len(self.sent)],
            recv_sem=self.recv.at[arrival],
            device_id=device,
            device_id_type=MESH,
        )
        copy.start()
        self.sent.append(copy)

    def arrive(self, dst, arrival, device):
        pltpu.make_async_remote_copy(
            src_ref=dst,
            dst_ref=dst,
            send_sem=self.send.at[0],
            recv_sem=self.recv.at[arrival],
            device_id=device,
            device_id_type=MESH,
        ).wait_recv()


def exchange(
    sims, helps, meta, ext_out, tiles_out, meta_out,
    ext, first, passing, second, metas,
    send, recv, rim_send, rim_recv, local_sem,
):
    n, g = lax.axis_index("nbr"), lax.axis_index("grp")
    groups = lax.axis_size("grp")
    x, z = n // SIDE, lax.rem(n, SIDE)
    blocks = sims.shape[0]
    total = ext.shape[0]

    def place(origin):
        return lax.rem(x + origin[0] + SIDE, SIDE) * SIDE + lax.rem(z + origin[1] + SIDE, SIDE)

    def step(axis, way):
        return (way, 0) if axis == 0 else (0, way)

    def neighbour(axis, way):
        return {"nbr": place(step(axis, way))}

    barrier = pltpu.get_barrier_semaphore()
    for axis in (0, 1):
        for way in (1, -1):
            pl.semaphore_signal(barrier, inc=1, device_id=neighbour(axis, way), device_id_type=MESH)

    @pl.when(g > 0)
    def _():
        pl.semaphore_signal(barrier, inc=1, device_id={"grp": g - 1}, device_id_type=MESH)

    @pl.when(g < groups - 1)
    def _():
        pl.semaphore_signal(barrier, inc=1, device_id={"grp": g + 1}, device_id_type=MESH)

    mine = pltpu.make_async_copy(sims, ext.at[pl.ds(RIM + n * blocks, blocks)], local_sem.at[0])
    mine.start()
    note = pltpu.make_async_copy(meta, metas.at[n], local_sem.at[1])
    note.start()
    bundles = [
        pltpu.make_async_copy(helps.at[x, :, 0], first.at[0, 0], local_sem.at[2]),
        pltpu.make_async_copy(helps.at[:, z, 1], first.at[1, 0], local_sem.at[3]),
    ]
    for bundle in bundles:
        bundle.start()

    @pl.when(g == 0)
    def _():
        ext[:RIM] = jnp.zeros((RIM,) + ext.shape[1:], ext.dtype)

    @pl.when(g == groups - 1)
    def _():
        ext[total - RIM :] = jnp.zeros((RIM,) + ext.shape[1:], ext.dtype)

    pl.semaphore_wait(
        barrier, 4 + (g > 0).astype(jnp.int32) + (g < groups - 1).astype(jnp.int32)
    )
    mine.wait()
    note.wait()
    link = Link(send, recv)

    def quarter(origin, sub):
        return ext.at[pl.ds(RIM + place(origin) * blocks + sub * UNIT, UNIT)]

    here = {unit_id((0, 0), sub) for sub in range(4)}

    def need(origin, sub):
        name = unit_id(origin, sub)
        if name not in here:
            here.add(name)
            link.arrive(quarter(origin, sub), name, neighbour(0, 1))

    queues = gather_queues()
    base = 64

    def note_row(dx):
        return metas.at[lax.rem(x + dx + SIDE, SIDE) * SIDE + z]

    def note_wait(ref, arrival):
        link.arrive(ref, arrival, neighbour(0, 1))

    for turn in range(len(queues[0][2])):
        for axis, way, queue in queues:
            origin, sub = queue[turn]
            need(origin, sub)
            seen = (origin[0] - step(axis, way)[0], origin[1] - step(axis, way)[1])
            link.start(
                quarter(origin, sub), quarter(origin, sub), unit_id(seen, sub), neighbour(axis, way)
            )
        if turn == 0:
            link.start(note_row(0), note_row(0), base, neighbour(0, 1))
            link.start(note_row(0), note_row(0), base + 1, neighbour(0, -1))
        if turn == 3:
            note_wait(note_row(-1), base)
            note_wait(note_row(1), base + 1)
            link.start(note_row(-1), note_row(-1), base + 2, neighbour(0, 1))
        if turn == 6:
            note_wait(note_row(2), base + 2)
            for dx in range(SIDE):
                link.start(note_row(dx), note_row(dx), base + 3 + dx, neighbour(1, 1))
                link.start(note_row(dx), note_row(dx), base + 7 + dx, neighbour(1, -1))
        if turn == 9:
            for dx in range(SIDE):
                behind = metas.at[place((dx, -1))]
                note_wait(behind, base + 3 + dx)
                note_wait(metas.at[place((dx, 1))], base + 7 + dx)
                link.start(behind, behind, base + 11 + dx, neighbour(1, 1))
    for dx in range(SIDE):
        note_wait(metas.at[place((dx, 2))], base + 11 + dx)
    base += 15
    for bundle in bundles:
        bundle.wait()

    def bundle_of(slot, to):
        at = place(to)
        return helps.at[at // SIDE, :, 0] if slot == 0 else helps.at[:, lax.rem(at, SIDE), 1]

    def pair_of(slot, to, low):
        at = place(to)
        part = pl.ds(low, 2)
        return helps.at[at // SIDE, part, 0] if slot == 0 else helps.at[part, lax.rem(at, SIDE), 1]

    def final(slot, along, across):
        dx, dz = (along % SIDE, across % SIDE) if slot == 0 else (across % SIDE, along % SIDE)
        return tiles_out.at[slot, dx, dz]

    def arrival(slot, kind):
        return base + slot * 28 + kind

    def target(slot, way):
        axis = 1 - slot
        at = place(step(axis, way))
        return lax.rem(at, SIDE) if axis == 1 else at // SIDE

    def opening(slot):
        for way, low in ((1, 0), (-1, 2)):
            k = 0 if way > 0 else 1
            link.start(
                pair_of(slot, step(slot, 2), low), passing.at[slot, k], arrival(slot, k),
                neighbour(slot, way),
            )
            link.start(
                bundle_of(slot, step(slot, way)), first.at[slot, -way % SIDE],
                arrival(slot, 2 + k), neighbour(slot, way),
            )

    def relay(slot):
        for way, low in ((1, 0), (-1, 2)):
            k = 0 if way > 0 else 1
            note_wait(passing.at[slot, k], arrival(slot, k))
            link.start(
                passing.at[slot, k], first.at[slot, 2, pl.ds(low, 2)], arrival(slot, 4 + k),
                neighbour(slot, way),
            )

    def direct(slot, along):
        for way in (1, -1):
            link.start(
                first.at[slot, along % SIDE, target(slot, way)], final(slot, along, -way),
                arrival(slot, 6 + (along % SIDE) * 4 + (-way) % SIDE), neighbour(1 - slot, way),
            )

    by = {0: 1, 1: 1, 3: -1, 2: -1}

    def detour(slot, along):
        way = by[along % SIDE]
        link.start(
            first.at[slot, along % SIDE, target(slot, 2)], second.at[slot, along % SIDE],
            arrival(slot, 22 + along % SIDE), neighbour(1 - slot, way),
        )

    def hand_on(slot, along):
        way = by[along % SIDE]
        note_wait(second.at[slot, along % SIDE], arrival(slot, 22 + along % SIDE))
        link.start(
            second.at[slot, along % SIDE], final(slot, along, 2),
            arrival(slot, 6 + (along % SIDE) * 4 + 2), neighbour(1 - slot, way),
        )

    def bundle_wait(slot, way):
        k = 0 if way > 0 else 1
        note_wait(first.at[slot, -way % SIDE], arrival(slot, 2 + k))

    slots = (0, 1)
    for slot in slots:
        opening(slot)
    for slot in slots:
        detour(slot, 0)
        direct(slot, 0)

    for a in range(SIDE):
        for b in range(SIDE):
            for sub in range(4):
                need((a, b), sub)
    up = pltpu.make_async_remote_copy(
        src_ref=ext.at[pl.ds(total - 2 * RIM, RIM)], dst_ref=ext.at[pl.ds(0, RIM)],
        send_sem=rim_send.at[0], recv_sem=rim_recv.at[0],
        device_id={"grp": lax.rem(g + 1, groups)}, device_id_type=MESH,
    )
    down = pltpu.make_async_remote_copy(
        src_ref=ext.at[pl.ds(RIM, RIM)], dst_ref=ext.at[pl.ds(total - RIM, RIM)],
        send_sem=rim_send.at[1], recv_sem=rim_recv.at[1],
        device_id={"grp": lax.rem(g + groups - 1, groups)}, device_id_type=MESH,
    )

    @pl.when(g < groups - 1)
    def _():
        up.start()

    @pl.when(g > 0)
    def _():
        down.start()

    for slot in slots:
        relay(slot)
    for slot in slots:
        for way in (1, -1):
            bundle_wait(slot, way)
    for slot in slots:
        direct(slot, -1)
        direct(slot, 1)
        detour(slot, 1)
        detour(slot, -1)

    @pl.when(g > 0)
    def _():
        up.wait_recv()

    @pl.when(g < groups - 1)
    def _():
        down.wait_recv()

    out = pltpu.make_async_copy(ext, ext_out, local_sem.at[0])
    out.start()
    notes = pltpu.make_async_copy(metas, meta_out, local_sem.at[1])
    notes.start()
    for slot in slots:
        hand_on(slot, 0)
        for k, low in ((0, 0), (1, 2)):
            note_wait(first.at[slot, 2, pl.ds(low, 2)], arrival(slot, 4 + k))
        detour(slot, 2)
        direct(slot, 2)
    stay = [
        pltpu.make_async_copy(first.at[0, :, z], tiles_out.at[0, :, 0], local_sem.at[2]),
        pltpu.make_async_copy(first.at[1, :, x], tiles_out.at[1, 0, :], local_sem.at[3]),
    ]
    for copy in stay:
        copy.start()
    for slot in slots:
        hand_on(slot, 1)
        hand_on(slot, -1)
    for slot in slots:
        hand_on(slot, 2)
    for slot in slots:
        for along in range(SIDE):
            for across in (1, 2, 3):
                note_wait(final(slot, along, across), arrival(slot, 6 + along * 4 + across))
    for copy in link.sent:
        copy.wait_send()

    @pl.when(g < groups - 1)
    def _():
        up.wait_send()

    @pl.when(g > 0)
    def _():
        down.wait_send()

    out.wait()
    notes.wait()
    for copy in stay:
        copy.wait()


def split(value):
    high = value.astype(jnp.bfloat16)
    return high, (value - high.astype(jnp.float32)).astype(jnp.bfloat16)


def product(tile, block):
    tile_parts = jnp.concatenate(split(tile), axis=1)
    block_parts = jnp.concatenate(split(block), axis=1)
    both = jnp.dot(
        tile_parts, jnp.concatenate([block_parts, block_parts], axis=0),
        preferred_element_type=jnp.float32,
    )
    return both[:, : block.shape[1]] + both[:, block.shape[1] :]


def products(
    own_cols, own_rows, notes, ext, own_tiles, help_tiles, total, tiles, blocks, tile_sem, block_sem
):
    n = lax.axis_index("nbr")
    x, z = n // SIDE, lax.rem(n, SIDE)
    n_own, n_help = own_tiles.shape[0], help_tiles.shape[0]
    total[...] = jnp.zeros_like(total)

    def copies(src, index, col):
        at = lax.rem(index, DEPTH)
        return (
            pltpu.make_async_copy(src.at[index], tiles.at[at], tile_sem.at[at]),
            pltpu.make_async_copy(ext.at[col], blocks.at[at], block_sem.at[at]),
        )

    def run(count, src, of):
        def fetch(index):
            col, _, live = of(index)

            @pl.when(live > 0)
            def _():
                for copy in copies(src, index, col):
                    copy.start()

        for index in range(DEPTH - 1):
            fetch(index)

        @pl.loop(0, count)
        def _(index):
            @pl.when(index + DEPTH - 1 < count)
            def _():
                fetch(index + DEPTH - 1)

            col, row, live = of(index)

            @pl.when(live > 0)
            def _():
                for copy in copies(src, index, col):
                    copy.wait()
                at = lax.rem(index, DEPTH)
                total[row] += product(tiles[at], blocks[at])

    def own(index):
        return own_cols[index], own_rows[index], 1

    def helper(index):
        slot, dx, dz = index // 16, lax.rem(index // SIDE, SIDE), lax.rem(index, SIDE)
        source = lax.rem(x + dx, SIDE) * SIDE + lax.rem(z + dz, SIDE)
        at = n * 2 + slot
        return notes[source, 0, at], notes[source, 1, at], notes[source, 2, at]

    run(n_own, own_tiles, own)
    run(n_help, help_tiles, helper)


def local(sims, own_tiles, own_cols, own_rows, help_tiles, help_cols, help_rows, help_live):
    blocks, size = sims.shape[0], sims.shape[1:]
    neighbours = lax.axis_size("nbr")
    helps = help_tiles.shape[0]
    extended = blocks * neighbours + 2 * RIM
    any_space = pl.BlockSpec(memory_space=pl.ANY)
    smem = pl.BlockSpec(memory_space=pltpu.SMEM)
    meta = jnp.pad(
        jnp.stack([help_cols, help_rows, help_live]), ((0, 5), (0, 128 - helps))
    )
    ext, tiles, notes = pl.pallas_call(
        exchange,
        out_shape=(
            jax.ShapeDtypeStruct((extended,) + size, jnp.float32),
            jax.ShapeDtypeStruct((2, SIDE, SIDE) + size, jnp.float32),
            jax.ShapeDtypeStruct((neighbours, 8, 128), jnp.int32),
        ),
        in_specs=[any_space] * 3,
        out_specs=(any_space,) * 3,
        scratch_shapes=[
            pltpu.VMEM((extended,) + size, jnp.float32),
            pltpu.VMEM((2, SIDE, SIDE) + size, jnp.float32),
            pltpu.VMEM((2, 2, 2) + size, jnp.float32),
            pltpu.VMEM((2, SIDE) + size, jnp.float32),
            pltpu.VMEM((neighbours, 8, 128), jnp.int32),
            pltpu.SemaphoreType.DMA((160,)),
            pltpu.SemaphoreType.DMA((160,)),
            pltpu.SemaphoreType.DMA((2,)),
            pltpu.SemaphoreType.DMA((2,)),
            pltpu.SemaphoreType.DMA((4,)),
        ],
        compiler_params=pltpu.CompilerParams(
            collective_id=0, has_side_effects=True, vmem_limit_bytes=56 * 2**20
        ),
        name="exchange",
    )(sims, help_tiles.reshape((SIDE, SIDE, 2) + size), meta)
    return pl.pallas_call(
        products,
        out_shape=jax.ShapeDtypeStruct(sims.shape, jnp.float32),
        in_specs=[smem] * 3 + [any_space] * 3,
        out_specs=pl.BlockSpec(memory_space=pltpu.VMEM),
        scratch_shapes=[
            pltpu.VMEM((DEPTH,) + size, jnp.float32),
            pltpu.VMEM((DEPTH,) + size, jnp.float32),
            pltpu.SemaphoreType.DMA((DEPTH,)),
            pltpu.SemaphoreType.DMA((DEPTH,)),
        ],
        name="products",
    )(own_cols, own_rows, notes, ext, own_tiles, tiles.reshape((helps,) + size))


def solution(mesh):
    whole, flat = P(("grp", "nbr"), None, None), P(("grp", "nbr"))
    placed = (whole, whole, flat, flat, whole, flat, flat, flat)
    return jax.shard_map(local, mesh=mesh, in_specs=placed, out_specs=whole, check_vma=False)
```

time: 254 us -> 165 us (0.65)
  Pallas kernels: 0 us -> 161 us
  waiting for transfers between devices: 106 us -> 0 us
  local copies, waits for them, and re-layouts: 60.1 us -> 0.6 us
  matrix products: 51.8 us -> 0 us
  starting transfers between devices: 19.1 us -> 0 us
  between operations: 13.5 us -> 0.01 us
    pallas_call x0 -> x2, Pallas kernels: none -> 161 us  [the longest x1 118 us: local(): pl.pallas_call(exchange, out_shape=(jax.ShapeDtypeStruct((extended,) + si...]
    all_gather x1 -> x0, waiting for transfers between devices: 105 us -> none  [local(): group = lax.all_gather(sims, 'nbr', axis=0, tiled=True)]
    dot_general x4 -> x0, matrix products: 51.8 us -> none  [the longest x1 33.9 us: local(): own_terms = jnp.einsum('tij,tjs->tis', own_tiles, own_pick, precision=high)]
    gather x6 -> x0, local copies, waits for them, and re-layouts: 40.1 us -> none  [pick_from(): taken = jnp.take(source, jnp.clip(index, 0, length - 1), axis=0)]
    all_to_all x2 -> x0, starting transfers between devices: 13.4 us -> none  [the longest x1 8.42 us: local(): lax.all_to_all(out_rows, 'nbr', split_axis=0, concat_axis=0, tiled=True)]
    dot_general x1 -> x0, local copies, waits for them, and re-layouts: 12.7 us -> none  [local(): own_terms = jnp.einsum('tij,tjs->tis', own_tiles, own_pick, precision=high)]
    ppermute x2 -> x0, starting transfers between devices: 5.75 us -> none  [the longest x1 3.83 us: padded(): before = lax.ppermute(last, axis, up)]
    all_to_all x3 -> x0, local copies, waits for them, and re-layouts: 3.62 us -> none  [the longest x1 2.45 us: local(): lax.all_to_all(outgoing, 'nbr', split_axis=0, concat_axis=0, tiled=True)]
  transfers between devices with their start and end apart: 5 -> 0, of which waited for: 1 -> 0; matrix products, arithmetic and copies ran while one was open for 38% -> 0% of each run, Pallas kernels for 0% -> 0%
where the time goes in v1:
time: 165 us; the launch traced here: 163 us
  Pallas kernels  161 us (98%)
    pallas_call x1, Pallas kernels, local(): pl.pallas_call(exchange, out_shape=(jax.ShapeDtypeStruct((extended,) + si...  118 us
    pallas_call x1, Pallas kernels, local(): pl.pallas_call(products, out_shape=jax.ShapeDtypeStruct(sims.shape, jnp.f...  42.9 us

profile of v1, /device:TPU:1, one launch (start us, length us, event | category | flops | bytes accessed | tf_op | source)
XLA Modules:
  0.0 162.6 jit_solution(12007303342508744239)
XLA Ops:
  0.0 0.7 pad_add_fusion
  0.7 0.6 pad.4.meta
  1.3 118.4 %exchange.1 = (f32[272,128,128]{2,1,0:T(8,128)}, f32[2,4,4,128,128]{4,3,2,1,0:T(8,128)}, s32[16,8,128]{2,1,0:T(8,128)}) custom-call(f32[16,128,128]{2,1,0:T(8,128)} %sims.1, f32[4,4,2,128,128]{4,3,2,1,0:T(8,128)} %bitcast.6, s32[8,128]{1,0:T(8,128)} %pad.4.meta), custom_call_target="tpu_custom_call" | custom-call | tf_op jit(solution)/shard_map/exchange/pallas_call | solution.py:432
  119.7 42.9 %products.1 = f32[16,128,128]{2,1,0:T(8,128)} custom-call(s32[192]{0:T(256)} %own_cols.1, s32[192]{0:T(256)} %own_rows.1, s32[16,8,128]{2,1,0:T(8,128)} %get-tuple-element.8.notes, f32[272,128,128]{2,1,0:T(8,128)} %get-tuple-element.9.ext, f32[192,128,128]{2,1,0:T(8,128)} %own_tiles.1, f32[32,128,128]{2,1,0:T(8,128)} %bitcast.5), custom_call_target="tpu_custom_call" | custom-call | tf_op jit(solution)/shard_map/products/pallas_call | solution.py:458

commit v2 on v1

v2 whole, which is shorter than its diff:
```python
import jax
import jax.numpy as jnp
from jax import lax
from jax.experimental import pallas as pl
from jax.experimental.pallas import tpu as pltpu
from jax.sharding import PartitionSpec as P

RIM = 8
UNIT = 4
SIDE = 4
UNROLL = 4
MESH = pl.DeviceIdType.MESH


def unit_id(origin, sub):
    return ((origin[0] % SIDE) * SIDE + origin[1] % SIDE) * 4 + sub


def gather_queues():
    queues = []
    for axis in (0, 1):
        for way in (1, -1):
            near, far = ((0, 1), (2, 3)) if axis == 0 else ((2, 3), (0, 1))
            if way < 0:
                near, far = near[::-1], far[::-1]

            def at(along, across, axis=axis):
                return (along, across) if axis == 0 else (across, along)

            queue = [
                (at(0, 0), near[0]),
                (at(0, 0), near[1]),
                (at(0, 0), far[0]),
                (at(-way, 0), near[0]),
                (at(0, 0), far[1]),
                (at(0, -1), far[0]),
                (at(0, 1), far[0]),
                (at(0, -1), far[1]),
                (at(0, 1), far[1]),
                (at(0, 2), far[0]),
                (at(0, 2), far[1]),
                (at(-way, 0), far[0]),
                (at(-way, -1), far[0]),
                (at(-way, 1), far[0]),
                (at(-way, 2), far[0]),
            ]
            queues.append((axis, way, queue))
    return queues


class Link:
    def __init__(self, send, recv):
        self.send, self.recv, self.sent = send, recv, []

    def start(self, src, dst, arrival, device):
        copy = pltpu.make_async_remote_copy(
            src_ref=src,
            dst_ref=dst,
            send_sem=self.send.at[len(self.sent)],
            recv_sem=self.recv.at[arrival],
            device_id=device,
            device_id_type=MESH,
        )
        copy.start()
        self.sent.append(copy)

    def arrive(self, dst, arrival, device):
        pltpu.make_async_remote_copy(
            src_ref=dst,
            dst_ref=dst,
            send_sem=self.send.at[0],
            recv_sem=self.recv.at[arrival],
            device_id=device,
            device_id_type=MESH,
        ).wait_recv()


def split(value):
    high = value.astype(jnp.bfloat16)
    low = (value - high.astype(jnp.float32)).astype(jnp.bfloat16)
    return jnp.concatenate([high, low], axis=1)


def product(tile, block):
    both = jnp.dot(
        tile, jnp.concatenate([block, block], axis=0), preferred_element_type=jnp.float32
    )
    half = both.shape[1] // 2
    return both[:, :half] + both[:, half:]


def order_table(cols, rows, table):
    count = rows.shape[1]
    table[...] = jnp.zeros_like(table)
    line = lax.broadcasted_iota(jnp.int32, (count, count), 1)
    deep = lax.broadcasted_iota(jnp.int32, (count, count), 0)

    def upright(value):
        return jnp.sum(jnp.where(line == deep, value, 0), axis=1, keepdims=True)

    key = rows * 256 + line[:1]
    key_up, col_up = upright(key), upright(cols)
    row_up = jnp.right_shift(key_up, 8)
    rank = jnp.sum((key < key_up).astype(jnp.int32), axis=1, keepdims=True)
    here = rank == line
    before = rank == line - 1
    row_at = jnp.sum(jnp.where(here, row_up, 0), axis=0, keepdims=True)
    row_before = jnp.sum(jnp.where(before, row_up + 1, 0), axis=0, keepdims=True) - 1
    table[0:1, :count] = jnp.sum(jnp.where(here, deep, 0), axis=0, keepdims=True)
    table[1:2, :count] = jnp.sum(jnp.where(here, col_up, 0), axis=0, keepdims=True)
    table[2:3, :count] = (row_at == row_before).astype(jnp.int32)
    upto = jnp.sum((row_up <= line).astype(jnp.int32), axis=0, keepdims=True)
    table[3:4, :count] = jnp.maximum(upto - 1, 0)
    table[4:5, :count] = jnp.minimum(
        jnp.sum((row_up == line).astype(jnp.int32), axis=0, keepdims=True), 1
    )


HELP_ORDER = (
    [(0, 0), (1, 0), (3, 0), (0, 1), (0, 3), (2, 0)]
    + [(1, 1), (1, 3), (3, 1), (3, 3), (0, 2), (1, 2), (3, 2)]
    + [(2, 1), (2, 3), (2, 2)]
)


def exchange(
    sims, helps, tiles, own_cols, own_rows, help_cols, help_rows, help_live,
    sums_out, terms_out, notes_out,
    ext, ext_parts, tile_parts, stage, first, passing, second, arrived, terms, sums,
    metas, vec, table, order, notes,
    send, recv, rim_send, rim_recv, local_sem, stage_sem,
):
    n, g = lax.axis_index("nbr"), lax.axis_index("grp")
    groups = lax.axis_size("grp")
    x, z = n // SIDE, lax.rem(n, SIDE)
    blocks = sims.shape[0]
    total = ext.shape[0]
    n_own = tiles.shape[0]
    last = SIDE * SIDE - 1

    def place(origin):
        return lax.rem(x + origin[0] + SIDE, SIDE) * SIDE + lax.rem(z + origin[1] + SIDE, SIDE)

    def step(axis, way):
        return (way, 0) if axis == 0 else (0, way)

    def neighbour(axis, way):
        return {"nbr": place(step(axis, way))}

    barrier = pltpu.get_barrier_semaphore()
    for axis in (0, 1):
        for way in (1, -1):
            pl.semaphore_signal(barrier, inc=1, device_id=neighbour(axis, way), device_id_type=MESH)

    @pl.when(g > 0)
    def _():
        pl.semaphore_signal(barrier, inc=1, device_id={"grp": g - 1}, device_id_type=MESH)

    @pl.when(g < groups - 1)
    def _():
        pl.semaphore_signal(barrier, inc=1, device_id={"grp": g + 1}, device_id_type=MESH)

    def fetch(src, dst, k):
        copy = pltpu.make_async_copy(src, dst, local_sem.at[k])
        copy.start()
        return copy

    mine = fetch(sims, ext.at[pl.ds(RIM + n * blocks, blocks)], 0)
    told = [
        fetch(ref, metas.at[n, k], 1 + k) for k, ref in enumerate((help_cols, help_rows, help_live))
    ]
    bundles = [
        fetch(helps.at[x, :, 0], first.at[0, 0], 4), fetch(helps.at[:, z, 1], first.at[1, 0], 5)
    ]
    vectors = [fetch(own_cols, vec.at[0], 6), fetch(own_rows, vec.at[1], 7)]

    def load(chunk):
        at = lax.rem(chunk, 2)
        return pltpu.make_async_copy(
            tiles.at[pl.ds(chunk * UNIT, UNIT)], stage.at[at], stage_sem.at[at]
        )

    for chunk in (0, 1):
        load(chunk).start()

    pl.semaphore_wait(
        barrier, 4 + (g > 0).astype(jnp.int32) + (g < groups - 1).astype(jnp.int32)
    )
    mine.wait()
    for copy in told:
        copy.wait()
    link = Link(send, recv)

    def split_unit(start):
        @pl.loop(0, UNIT)
        def _(k):
            ext_parts[start + k] = split(ext[start + k])

    def split_tiles(low, high):
        @pl.loop(low, high)
        def _(chunk):
            load(chunk).wait()
            at = lax.rem(chunk, 2)

            @pl.loop(0, UNIT)
            def _(k):
                tile_parts[chunk * UNIT + k] = split(stage[at, k])

            @pl.when(chunk + 2 < n_own // UNIT)
            def _():
                load(chunk + 2).start()

    def rim_copy(piece):
        up = piece < 2
        src = total - 2 * RIM + piece * UNIT if up else RIM + (piece - 2) * UNIT
        dst = piece * UNIT if up else total - RIM + (piece - 2) * UNIT
        peer = lax.rem(g + 1, groups) if up else lax.rem(g + groups - 1, groups)
        return pltpu.make_async_remote_copy(
            src_ref=ext.at[pl.ds(src, UNIT)], dst_ref=ext.at[pl.ds(dst, UNIT)],
            send_sem=rim_send.at[piece], recv_sem=rim_recv.at[piece],
            device_id={"grp": peer}, device_id_type=MESH,
        )

    def rim_leaves(origin, sub):
        at = place(origin)
        sends = (at == last) & (g < groups - 1) if sub >= 2 else (at == 0) & (g > 0)

        @pl.when(sends)
        def _():
            rim_copy(sub - 2 if sub >= 2 else sub + 2).start()

    def base_of(origin, sub):
        return RIM + place(origin) * blocks + sub * UNIT

    def quarter(origin, sub):
        return ext.at[pl.ds(base_of(origin, sub), UNIT)]

    here = set()
    fresh = []

    def need(origin, sub):
        name = unit_id(origin, sub)
        if name in here:
            return
        here.add(name)
        fresh.append((origin, sub))
        if name >= 4:
            link.arrive(quarter(origin, sub), name, neighbour(0, 1))

    def tidy():
        for origin, sub in fresh:
            rim_leaves(origin, sub)
        for origin, sub in fresh:
            split_unit(base_of(origin, sub))
        fresh.clear()

    base = 64

    def note_row(dx):
        return metas.at[lax.rem(x + dx + SIDE, SIDE) * SIDE + z]

    def note_wait(ref, arrival):
        link.arrive(ref, arrival, neighbour(0, 1))

    queues = gather_queues()
    turns = len(queues[0][2])
    chunks = n_own // UNIT
    for turn in range(turns):
        for axis, way, queue in queues:
            origin, sub = queue[turn]
            need(origin, sub)
            seen = (origin[0] - step(axis, way)[0], origin[1] - step(axis, way)[1])
            link.start(
                quarter(origin, sub), quarter(origin, sub), unit_id(seen, sub), neighbour(axis, way)
            )
        if turn == 0:
            link.start(note_row(0), note_row(0), base, neighbour(0, 1))
            link.start(note_row(0), note_row(0), base + 1, neighbour(0, -1))
        if turn == 3:
            note_wait(note_row(-1), base)
            note_wait(note_row(1), base + 1)
            link.start(note_row(-1), note_row(-1), base + 2, neighbour(0, 1))
        if turn == 6:
            note_wait(note_row(2), base + 2)
            for dx in range(SIDE):
                link.start(note_row(dx), note_row(dx), base + 3 + dx, neighbour(1, 1))
                link.start(note_row(dx), note_row(dx), base + 7 + dx, neighbour(1, -1))
        if turn == 9:
            for dx in range(SIDE):
                behind = metas.at[place((dx, -1))]
                note_wait(behind, base + 3 + dx)
                note_wait(metas.at[place((dx, 1))], base + 7 + dx)
                link.start(behind, behind, base + 11 + dx, neighbour(1, 1))
        tidy()
        if turn == 1:
            for copy in vectors:
                copy.wait()
            order_table(vec[0], vec[1], table)
            fetch(table, order, 6).wait()
        split_tiles(chunks * turn // turns, chunks * (turn + 1) // turns)
    of_ext = len(link.sent)
    for dx in range(SIDE):
        note_wait(metas.at[place((dx, 2))], base + 11 + dx)
    base += 15
    for bundle in bundles:
        bundle.wait()

    def bundle_of(slot, to):
        at = place(to)
        return helps.at[at // SIDE, :, 0] if slot == 0 else helps.at[:, lax.rem(at, SIDE), 1]

    def pair_of(slot, to, low):
        at = place(to)
        part = pl.ds(low, 2)
        return helps.at[at // SIDE, part, 0] if slot == 0 else helps.at[part, lax.rem(at, SIDE), 1]

    def final(slot, along, across):
        return arrived.at[slot, along % SIDE, across % SIDE - 1]

    def arrival(slot, kind):
        return base + slot * 28 + kind

    def target(slot, way):
        axis = 1 - slot
        at = place(step(axis, way))
        return lax.rem(at, SIDE) if axis == 1 else at // SIDE

    def opening(slot):
        for way, low in ((1, 0), (-1, 2)):
            k = 0 if way > 0 else 1
            link.start(
                pair_of(slot, step(slot, 2), low), passing.at[slot, k], arrival(slot, k),
                neighbour(slot, way),
            )
            link.start(
                bundle_of(slot, step(slot, way)), first.at[slot, -way % SIDE],
                arrival(slot, 2 + k), neighbour(slot, way),
            )

    def relay(slot):
        for way, low in ((1, 0), (-1, 2)):
            k = 0 if way > 0 else 1
            note_wait(passing.at[slot, k], arrival(slot, k))
            link.start(
                passing.at[slot, k], first.at[slot, 2, pl.ds(low, 2)], arrival(slot, 4 + k),
                neighbour(slot, way),
            )

    def direct(slot, along):
        for way in (1, -1):
            link.start(
                first.at[slot, along % SIDE, target(slot, way)], final(slot, along, -way),
                arrival(slot, 6 + (along % SIDE) * 4 + (-way) % SIDE), neighbour(1 - slot, way),
            )

    by = {0: 1, 1: 1, 3: -1, 2: -1}

    def detour(slot, along):
        way = by[along % SIDE]
        link.start(
            first.at[slot, along % SIDE, target(slot, 2)], second.at[slot, along % SIDE],
            arrival(slot, 22 + along % SIDE), neighbour(1 - slot, way),
        )

    def hand_on(slot, along):
        way = by[along % SIDE]
        note_wait(second.at[slot, along % SIDE], arrival(slot, 22 + along % SIDE))
        link.start(
            second.at[slot, along % SIDE], final(slot, along, 2),
            arrival(slot, 6 + (along % SIDE) * 4 + 2), neighbour(1 - slot, way),
        )

    def bundle_wait(slot, way):
        k = 0 if way > 0 else 1
        note_wait(first.at[slot, -way % SIDE], arrival(slot, 2 + k))

    slots = (0, 1)
    for slot in slots:
        opening(slot)
    for slot in slots:
        detour(slot, 0)
        direct(slot, 0)
    scalars = fetch(metas, notes, 1)
    notes_copy = fetch(metas, notes_out, 2)

    for a in range(SIDE):
        for b in range(SIDE):
            for sub in range(4):
                need((a, b), sub)
    tidy()

    def rim(has, pieces, start):
        @pl.when(has)
        def _():
            for piece in pieces:
                rim_copy(piece).wait_recv()
            for k in range(RIM // UNIT):
                split_unit(start + k * UNIT)

        @pl.when(jnp.logical_not(has))
        def _():
            ext_parts[start : start + RIM] = jnp.zeros((RIM,) + ext_parts.shape[1:], jnp.bfloat16)

    rim(g > 0, (0, 1), 0)
    rim(g < groups - 1, (2, 3), total - RIM)
    for copy in link.sent[:of_ext]:
        copy.wait_send()

    @pl.when(g < groups - 1)
    def _():
        for piece in (0, 1):
            rim_copy(piece).wait_send()

    @pl.when(g > 0)
    def _():
        for piece in (2, 3):
            rim_copy(piece).wait_send()

    def own(low, high):
        def body(k, acc):
            for u in range(UNROLL):
                at = low + k * UNROLL + u
                keep = order[2, at].astype(jnp.float32)
                acc = acc * keep + product(tile_parts[order[0, at]], ext_parts[order[1, at]])
                ext[at] = acc
            return acc

        acc = jnp.zeros(ext.shape[1:], jnp.float32) if low == 0 else ext[low - 1]
        lax.fori_loop(0, (high - low) // UNROLL, body, acc)

    def help_product(k, slot):
        along, across = HELP_ORDER[k]
        if across == 0:
            tile = first[slot, along, target(slot, 0)]
        else:
            note_wait(final(slot, along, across), arrival(slot, 6 + along * 4 + across))
            tile = arrived[slot, along, across - 1]
        source = place((along, across) if slot == 0 else (across, along))
        col = notes[source, 0, 0, n * 2 + slot]
        terms[k * 2 + slot] = product(split(tile), ext_parts[col])

    def help_products(low, high):
        for k in range(low, high):
            for slot in slots:
                help_product(k, slot)

    quart = n_own // 4
    own(0, quart)
    for slot in slots:
        relay(slot)
    own(quart, 2 * quart)
    for slot in slots:
        for way in (1, -1):
            bundle_wait(slot, way)
    for slot in slots:
        direct(slot, -1)
        direct(slot, 1)
        detour(slot, 1)
        detour(slot, -1)
    own(2 * quart, 3 * quart)
    for slot in slots:
        hand_on(slot, 0)
    own(3 * quart, n_own)

    @pl.loop(0, blocks)
    def _(row):
        sums[row] = ext[order[3, row]] * order[4, row].astype(jnp.float32)

    sums_copy = fetch(sums, sums_out, 3)
    scalars.wait()
    for slot in slots:
        for k, low in ((0, 0), (1, 2)):
            note_wait(first.at[slot, 2, pl.ds(low, 2)], arrival(slot, 4 + k))
        detour(slot, 2)
        direct(slot, 2)
    help_products(0, 3)
    for slot in slots:
        hand_on(slot, 1)
        hand_on(slot, -1)
    help_products(3, 8)
    for slot in slots:
        hand_on(slot, 2)
    help_products(8, 13)
    early = 26
    terms_copy = fetch(terms.at[pl.ds(0, early)], terms_out.at[pl.ds(0, early)], 4)
    help_products(13, 16)
    rest = terms.shape[0] - early
    rest_copy = fetch(terms.at[pl.ds(early, rest)], terms_out.at[pl.ds(early, rest)], 5)
    for copy in link.sent[of_ext:]:
        copy.wait_send()
    for copy in (notes_copy, sums_copy, terms_copy, rest_copy):
        copy.wait()


def add_terms(notes_in, sums, terms_in, total, terms, notes, sem):
    copies = [
        pltpu.make_async_copy(notes_in, notes, sem.at[0]),
        pltpu.make_async_copy(sums, total, sem.at[1]),
        pltpu.make_async_copy(terms_in, terms, sem.at[2]),
    ]
    for copy in copies:
        copy.start()
    n = lax.axis_index("nbr")
    x, z = n // SIDE, lax.rem(n, SIDE)
    for copy in copies:
        copy.wait()
    for k, (along, across) in enumerate(HELP_ORDER):
        for slot in (0, 1):
            dx, dz = (along, across) if slot == 0 else (across, along)
            source = lax.rem(x + dx, SIDE) * SIDE + lax.rem(z + dz, SIDE)
            at = n * 2 + slot
            row, live = notes[source, 1, 0, at], notes[source, 2, 0, at]
            total[row] += terms[k * 2 + slot] * live.astype(jnp.float32)


def local(sims, own_tiles, own_cols, own_rows, help_tiles, help_cols, help_rows, help_live):
    blocks, size = sims.shape[0], sims.shape[1:]
    neighbours = lax.axis_size("nbr")
    helps, owns = help_tiles.shape[0], own_tiles.shape[0]
    extended = blocks * neighbours + 2 * RIM
    parts = (size[0], 2 * size[1])
    any_space = pl.BlockSpec(memory_space=pl.ANY)
    f32, bf16, i32 = jnp.float32, jnp.bfloat16, jnp.int32
    sums, terms, notes = pl.pallas_call(
        exchange,
        out_shape=(
            jax.ShapeDtypeStruct(sims.shape, f32),
            jax.ShapeDtypeStruct(help_tiles.shape, f32),
            jax.ShapeDtypeStruct((neighbours, 3, 1, helps), i32),
        ),
        in_specs=[any_space] * 8,
        out_specs=(any_space,) * 3,
        scratch_shapes=[
            pltpu.VMEM((extended,) + size, f32),
            pltpu.VMEM((extended,) + parts, bf16),
            pltpu.VMEM((owns,) + parts, bf16),
            pltpu.VMEM((2, UNIT) + size, f32),
            pltpu.VMEM((2, SIDE, SIDE) + size, f32),
            pltpu.VMEM((2, 2, 2) + size, f32),
            pltpu.VMEM((2, SIDE) + size, f32),
            pltpu.VMEM((2, SIDE, SIDE - 1) + size, f32),
            pltpu.VMEM((helps,) + size, f32),
            pltpu.VMEM(sims.shape, f32),
            pltpu.VMEM((neighbours, 3, 1, helps), i32),
            pltpu.VMEM((2, 1, owns), i32),
            pltpu.VMEM((8, 256), i32),
            pltpu.SMEM((8, 256), i32),
            pltpu.SMEM((neighbours, 3, 1, helps), i32),
            pltpu.SemaphoreType.DMA((160,)),
            pltpu.SemaphoreType.DMA((160,)),
            pltpu.SemaphoreType.DMA((4,)),
            pltpu.SemaphoreType.DMA((4,)),
            pltpu.SemaphoreType.DMA((8,)),
            pltpu.SemaphoreType.DMA((2,)),
        ],
        compiler_params=pltpu.CompilerParams(
            collective_id=0, has_side_effects=True, vmem_limit_bytes=63 * 2**20
        ),
        name="exchange",
    )(
        sims,
        help_tiles.reshape((SIDE, SIDE, 2) + size),
        own_tiles,
        *(v.reshape(1, -1) for v in (own_cols, own_rows, help_cols, help_rows, help_live)),
    )
    return pl.pallas_call(
        add_terms,
        out_shape=jax.ShapeDtypeStruct(sims.shape, f32),
        in_specs=[any_space] * 3,
        out_specs=pl.BlockSpec(memory_space=pltpu.VMEM),
        scratch_shapes=[
            pltpu.VMEM(help_tiles.shape, f32),
            pltpu.SMEM((neighbours, 3, 1, helps), i32),
            pltpu.SemaphoreType.DMA((3,)),
        ],
        name="add_terms",
    )(notes, sums, terms)


def solution(mesh):
    whole, flat = P(("grp", "nbr"), None, None), P(("grp", "nbr"))
    placed = (whole, whole, flat, flat, whole, flat, flat, flat)
    return jax.shard_map(local, mesh=mesh, in_specs=placed, out_specs=whole, check_vma=False)
```

time: 165 us -> 127 us (0.77)
  Pallas kernels: 161 us -> 126 us
    pallas_call x2, Pallas kernels: 161 us -> 126 us  [the longest x1 123 us: local(): pl.pallas_call(exchange, out_shape=(jax.ShapeDtypeStruct(sims.shape, f32)...]
where the time goes in v2:
time: 127 us; the launch traced here: 126 us
  Pallas kernels  126 us (99%)
    pallas_call x1, Pallas kernels, local(): pl.pallas_call(exchange, out_shape=(jax.ShapeDtypeStruct(sims.shape, f32)...  123 us
    pallas_call x1, Pallas kernels, local(): pl.pallas_call(add_terms, out_shape=jax.ShapeDtypeStruct(sims.shape, f32)...  3.21 us

profile of v2, /device:TPU:1, one launch (start us, length us, event | category | flops | bytes accessed | tf_op | source)
XLA Modules:
  0.0 126.2 jit_solution(10938691175489403537)
XLA Ops:
  0.0 123.0 %exchange.1 = (f32[16,128,128]{2,1,0:T(8,128)}, f32[32,128,128]{2,1,0:T(8,128)}, s32[16,3,1,32]{3,2,1,0:T(1,128)}) custom-call(f32[16,128,128]{2,1,0:T(8,128)} %sims.1, f32[4,4,2,128,128]{4,3,2,1,0:T(8,128)} %bitcast.6, f32[192,128,128]{2,1,0:T(8,128)} %tiles.1, s32[1,192]{1,0:T(1,128)} %bitcast.7, s32[1,192]{1,0:T(1,128)} %bitcast.8, s32[1,32]{1,0:T(1,128)} %bitcast.9, ...), custom_call_target="tpu_custom_call" | custom-call | tf_op jit(solution)/shard_map/exchange/pallas_call | solution.py:524
  123.0 3.2 %add_terms.1 = f32[16,128,128]{2,1,0:T(8,128)} custom-call(s32[16,3,1,32]{3,2,1,0:T(1,128)} %get-tuple-element.8.notes_in, f32[16,128,128]{2,1,0:T(8,128)} %get-tuple-element.9.sums, f32[32,128,128]{2,1,0:T(8,128)} %get-tuple-element.10.terms_in), custom_call_target="tpu_custom_call" | custom-call | tf_op jit(solution)/shard_map/add_terms/pallas_call | solution.py:566

commit v3 on v2

--- a/solution.py
+++ b/solution.py
@@ -8,12 +8,16 @@
 RIM = 8
 UNIT = 4
 SIDE = 4
-UNROLL = 4
+UNROLL = 16
 MESH = pl.DeviceIdType.MESH
 
 
+def wrap(value):
+    return (value + SIDE) % SIDE if isinstance(value, int) else lax.rem(value + SIDE, SIDE)
+
+
 def unit_id(origin, sub):
-    return ((origin[0] % SIDE) * SIDE + origin[1] % SIDE) * 4 + sub
+    return (wrap(origin[0]) * SIDE + wrap(origin[1])) * 4 + sub
 
 
 def gather_queues():
@@ -39,12 +43,8 @@
                 (at(0, 1), far[1]),
                 (at(0, 2), far[0]),
                 (at(0, 2), far[1]),
-                (at(-way, 0), far[0]),
-                (at(-way, -1), far[0]),
-                (at(-way, 1), far[0]),
-                (at(-way, 2), far[0]),
             ]
-            queues.append((axis, way, queue))
+            queues.append((axis, way, queue, far[0]))
     return queues
 
 
@@ -117,17 +117,17 @@
 
 
 HELP_ORDER = (
-    [(0, 0), (1, 0), (3, 0), (0, 1), (0, 3), (2, 0)]
-    + [(1, 1), (1, 3), (3, 1), (3, 3), (0, 2), (1, 2), (3, 2)]
-    + [(2, 1), (2, 3), (2, 2)]
+    [(0, 0), (1, 0), (3, 0), (2, 0), (0, 1), (0, 3), (1, 1), (1, 3)]
+    + [(3, 1), (3, 3), (2, 1), (2, 3), (0, 2), (3, 2), (1, 2), (2, 2)]
 )
+LATE = 2
 
 
 def exchange(
     sims, helps, tiles, own_cols, own_rows, help_cols, help_rows, help_live,
-    sums_out, terms_out, notes_out,
+    sums_out,
     ext, ext_parts, tile_parts, stage, first, passing, second, arrived, terms, sums,
-    metas, vec, table, order, notes,
+    metas, vec, table, order, help_order, notes,
     send, recv, rim_send, rim_recv, local_sem, stage_sem,
 ):
     n, g = lax.axis_index("nbr"), lax.axis_index("grp")
@@ -262,11 +262,115 @@
     def note_wait(ref, arrival):
         link.arrive(ref, arrival, neighbour(0, 1))
 
+    def bundle_of(slot, to):
+        at = place(to)
+        return helps.at[at // SIDE, :, 0] if slot == 0 else helps.at[:, lax.rem(at, SIDE), 1]
+
+    def pair_of(slot, to, low):
+        at = place(to)
+        part = pl.ds(low, 2)
+        return helps.at[at // SIDE, part, 0] if slot == 0 else helps.at[part, lax.rem(at, SIDE), 1]
+
+    def final(slot, along, across):
+        return arrived.at[slot, along % SIDE, across % SIDE - 1]
+
+    def arrival(slot, kind):
+        return 79 + slot * 28 + kind
+
+    def target(slot, way):
+        axis = 1 - slot
+        at = place(step(axis, way))
+        return lax.rem(at, SIDE) if axis == 1 else at // SIDE
+
+    def far_pairs(slot):
+        for way, low in ((1, 0), (-1, 2)):
+            k = 0 if way > 0 else 1
+            link.start(
+                pair_of(slot, step(slot, 2), low), passing.at[slot, k], arrival(slot, k),
+                neighbour(slot, way),
+            )
+
+    def bundle(slot):
+        for way in (1, -1):
+            link.start(
+                bundle_of(slot, step(slot, way)), first.at[slot, -way % SIDE],
+                arrival(slot, 2 + (0 if way > 0 else 1)), neighbour(slot, way),
+            )
+
+    def relay(slot):
+        for way, low in ((1, 0), (-1, 2)):
+            k = 0 if way > 0 else 1
+            note_wait(passing.at[slot, k], arrival(slot, k))
+            link.start(
+                passing.at[slot, k], first.at[slot, 2, pl.ds(low, 2)], arrival(slot, 4 + k),
+                neighbour(slot, way),
+            )
+
+    def direct(slot, along):
+        for way in (1, -1):
+            link.start(
+                first.at[slot, along % SIDE, target(slot, way)], final(slot, along, -way),
+                arrival(slot, 6 + (along % SIDE) * 4 + (-way) % SIDE), neighbour(1 - slot, way),
+            )
+
+    by = {0: 1, 1: 1, 3: -1, 2: -1}
+
+    def detour(slot, along):
+        way = by[along % SIDE]
+        link.start(
+            first.at[slot, along % SIDE, target(slot, 2)], second.at[slot, along % SIDE],
+            arrival(slot, 22 + along % SIDE), neighbour(1 - slot, way),
+        )
+
+    def hand_on(slot, along):
+        way = by[along % SIDE]
+        note_wait(second.at[slot, along % SIDE], arrival(slot, 22 + along % SIDE))
+        link.start(
+            second.at[slot, along % SIDE], final(slot, along, 2),
+            arrival(slot, 6 + (along % SIDE) * 4 + 2), neighbour(1 - slot, way),
+        )
+
+    def bundle_wait(slot, way):
+        k = 0 if way > 0 else 1
+        note_wait(first.at[slot, -way % SIDE], arrival(slot, 2 + k))
+
+    slots = (0, 1)
+
+    def rim(has, pieces, start):
+        @pl.when(has)
+        def _():
+            for piece in pieces:
+                rim_copy(piece).wait_recv()
+            for k in range(RIM // UNIT):
+                split_unit(start + k * UNIT)
+
+        @pl.when(jnp.logical_not(has))
+        def _():
+            ext_parts[start : start + RIM] = jnp.zeros((RIM,) + ext_parts.shape[1:], jnp.bfloat16)
+
+    def noted(k, slot):
+        along, across = HELP_ORDER[k]
+        source = place((along, across) if slot == 0 else (across, along))
+        return [notes[source, kind, 0, n * 2 + slot] for kind in range(3)]
+
+    def list_rows():
+        spots = lax.broadcasted_iota(jnp.int32, (1, terms.shape[0]), 1)
+        help_rows_line = jnp.full_like(spots, blocks)
+        help_live_line = jnp.zeros_like(spots)
+        for k in range(len(HELP_ORDER) - LATE):
+            for slot in slots:
+                _, row, live = noted(k, slot)
+                help_rows_line = jnp.where(spots == k * 2 + slot, row, help_rows_line)
+                help_live_line = jnp.where(spots == k * 2 + slot, live, help_live_line)
+        order_table(help_live_line, help_rows_line, table)
+        help_table = fetch(table, help_order, 2)
+        return help_table
+
     queues = gather_queues()
     turns = len(queues[0][2])
     chunks = n_own // UNIT
     for turn in range(turns):
-        for axis, way, queue in queues:
+        for axis, way, queue, _ in queues:
             origin, sub = queue[turn]
             need(origin, sub)
             seen = (origin[0] - step(axis, way)[0], origin[1] - step(axis, way)[1])
@@ -291,6 +395,13 @@
                 note_wait(behind, base + 3 + dx)
                 note_wait(metas.at[place((dx, 1))], base + 7 + dx)
                 link.start(behind, behind, base + 11 + dx, neighbour(1, 1))
+        for slot in slots:
+            if turn == 5:
+                far_pairs(slot)
+            if turn == 8:
+                relay(slot)
+            if turn == turns - 1:
+                bundle(slot)
         tidy()
         if turn == 1:
             for copy in vectors:
@@ -298,109 +409,57 @@
             order_table(vec[0], vec[1], table)
             fetch(table, order, 6).wait()
         split_tiles(chunks * turn // turns, chunks * (turn + 1) // turns)
+
+    for axis, way, _, sub in queues:
+        for across in range(SIDE):
+            need((-way, across) if axis == 0 else (across, -way), sub)
+
+    def ahead(axis, k):
+        lead = SIDE - 1 - z if axis == 0 else SIDE - x
+        return lax.rem(lead + k, SIDE)
+
+    for k in range(SIDE):
+        for axis, way, _, sub in queues:
+            across = ahead(axis, k)
+            origin = (-way, across) if axis == 0 else (across, -way)
+            seen = (-2, across) if axis == 0 else (across, -2)
+            link.start(
+                quarter(origin, sub), quarter(origin, sub), unit_id(seen, sub), neighbour(axis, way)
+            )
     of_ext = len(link.sent)
-    for dx in range(SIDE):
-        note_wait(metas.at[place((dx, 2))], base + 11 + dx)
-    base += 15
-    for bundle in bundles:
-        bundle.wait()
-
-    def bundle_of(slot, to):
-        at = place(to)
-        return helps.at[at // SIDE, :, 0] if slot == 0 else helps.at[:, lax.rem(at, SIDE), 1]
-
-    def pair_of(slot, to, low):
-        at = place(to)
-        part = pl.ds(low, 2)
-        return helps.at[at // SIDE, part, 0] if slot == 0 else helps.at[part, lax.rem(at, SIDE), 1]
-
-    def final(slot, along, across):
-        return arrived.at[slot, along % SIDE, across % SIDE - 1]
-
-    def arrival(slot, kind):
-        return base + slot * 28 + kind
-
-    def target(slot, way):
-        axis = 1 - slot
-        at = place(step(axis, way))
-        return lax.rem(at, SIDE) if axis == 1 else at // SIDE
-
-    def opening(slot):
-        for way, low in ((1, 0), (-1, 2)):
-            k = 0 if way > 0 else 1
-            link.start(
-                pair_of(slot, step(slot, 2), low), passing.at[slot, k], arrival(slot, k),
-                neighbour(slot, way),
-            )
-            link.start(
-                bundle_of(slot, step(slot, way)), first.at[slot, -way % SIDE],
-                arrival(slot, 2 + k), neighbour(slot, way),
-            )
-
-    def relay(slot):
-        for way, low in ((1, 0), (-1, 2)):
-            k = 0 if way > 0 else 1
-            note_wait(passing.at[slot, k], arrival(slot, k))
-            link.start(
-                passing.at[slot, k], first.at[slot, 2, pl.ds(low, 2)], arrival(slot, 4 + k),
-                neighbour(slot, way),
-            )
-
-    def direct(slot, along):
-        for way in (1, -1):
-            link.start(
-                first.at[slot, along % SIDE, target(slot, way)], final(slot, along, -way),
-                arrival(slot, 6 + (along % SIDE) * 4 + (-way) % SIDE), neighbour(1 - slot, way),
-            )
-
-    by = {0: 1, 1: 1, 3: -1, 2: -1}
-
-    def detour(slot, along):
-        way = by[along % SIDE]
-        link.start(
-            first.at[slot, along % SIDE, target(slot, 2)], second.at[slot, along % SIDE],
-            arrival(slot, 22 + along % SIDE), neighbour(1 - slot, way),
-        )
-
-    def hand_on(slot, along):
-        way = by[along % SIDE]
-        note_wait(second.at[slot, along % SIDE], arrival(slot, 22 + along % SIDE))
-        link.start(
-            second.at[slot, along % SIDE], final(slot, along, 2),
-            arrival(slot, 6 + (along % SIDE) * 4 + 2), neighbour(1 - slot, way),
-        )
-
-    def bundle_wait(slot, way):
-        k = 0 if way > 0 else 1
-        note_wait(first.at[slot, -way % SIDE], arrival(slot, 2 + k))
-
-    slots = (0, 1)
-    for slot in slots:
-        opening(slot)
-    for slot in slots:
-        detour(slot, 0)
-        direct(slot, 0)
-    scalars = fetch(metas, notes, 1)
-    notes_copy = fetch(metas, notes_out, 2)
-
     for a in range(SIDE):
         for b in range(SIDE):
             for sub in range(4):
-                need((a, b), sub)
+                if not (a == 2 and sub >= 2 or b == 2 and sub < 2):
+                    need((a, b), sub)
     tidy()
-
-    def rim(has, pieces, start):
-        @pl.when(has)
-        def _():
-            for piece in pieces:
-                rim_copy(piece).wait_recv()
-            for k in range(RIM // UNIT):
-                split_unit(start + k * UNIT)
-
-        @pl.when(jnp.logical_not(has))
-        def _():
-            ext_parts[start : start + RIM] = jnp.zeros((RIM,) + ext_parts.shape[1:], jnp.bfloat16)
-
+    for copy in bundles:
+        copy.wait()
+
+    for slot in slots:
+        for k, low in ((0, 0), (1, 2)):
+            note_wait(first.at[slot, 2, pl.ds(low, 2)], arrival(slot, 4 + k))
+        for way in (1, -1):
+            bundle_wait(slot, way)
+    for along in (0, 3, 1, 2):
+        for slot in slots:
+            detour(slot, along)
+    for along in (0, 1, 3, 2):
+        for slot in slots:
+            direct(slot, along)
+    for dx in range(SIDE):
+        note_wait(metas.at[place((dx, 2))], base + 11 + dx)
+    fetch(metas, notes, 1).wait()
+
+    for k in range(SIDE):
+        for axis, way, _, sub in queues:
+            across = ahead(axis, k)
+            origin = (2, across) if axis == 0 else (across, 2)
+            link.arrive(quarter(origin, sub), unit_id(origin, sub), neighbour(0, 1))
+            fresh.append((origin, sub))
+        tidy()
+        if k == 0:
+            help_table = list_rows()
     rim(g > 0, (0, 1), 0)
     rim(g < groups - 1, (2, 3), total - RIM)
     for copy in link.sent[:of_ext]:
@@ -428,89 +487,63 @@
         acc = jnp.zeros(ext.shape[1:], jnp.float32) if low == 0 else ext[low - 1]
         lax.fori_loop(0, (high - low) // UNROLL, body, acc)
 
-    def help_product(k, slot):
-        along, across = HELP_ORDER[k]
-        if across == 0:
-            tile = first[slot, along, target(slot, 0)]
-        else:
-            note_wait(final(slot, along, across), arrival(slot, 6 + along * 4 + across))
-            tile = arrived[slot, along, across - 1]
-        source = place((along, across) if slot == 0 else (across, along))
-        col = notes[source, 0, 0, n * 2 + slot]
-        terms[k * 2 + slot] = product(split(tile), ext_parts[col])
-
     def help_products(low, high):
         for k in range(low, high):
+            along, across = HELP_ORDER[k]
             for slot in slots:
-                help_product(k, slot)
-
-    quart = n_own // 4
-    own(0, quart)
-    for slot in slots:
-        relay(slot)
-    own(quart, 2 * quart)
-    for slot in slots:
-        for way in (1, -1):
-            bundle_wait(slot, way)
-    for slot in slots:
-        direct(slot, -1)
-        direct(slot, 1)
-        detour(slot, 1)
-        detour(slot, -1)
-    own(2 * quart, 3 * quart)
-    for slot in slots:
-        hand_on(slot, 0)
-    own(3 * quart, n_own)
+                if across:
+                    note_wait(final(slot, along, across), arrival(slot, 6 + along * 4 + across))
+        for k in range(low, high):
+            along, across = HELP_ORDER[k]
+            for slot in slots:
+                tile = (
+                    arrived[slot, along, across - 1]
+                    if across
+                    else first[slot, along, target(slot, 0)]
+                )
+                terms[k * 2 + slot] = product(split(tile), ext_parts[noted(k, slot)[0]])
+
+    cut = n_own // 2
+    own(0, cut)
+    for along in (0, 3, 1, 2):
+        for slot in slots:
+            hand_on(slot, along)
+    own(cut, n_own)
 
     @pl.loop(0, blocks)
     def _(row):
         sums[row] = ext[order[3, row]] * order[4, row].astype(jnp.float32)
 
-    sums_copy = fetch(sums, sums_out, 3)
-    scalars.wait()
-    for slot in slots:
-        for k, low in ((0, 0), (1, 2)):
-            note_wait(first.at[slot, 2, pl.ds(low, 2)], arrival(slot, 4 + k))
-        detour(slot, 2)
-        direct(slot, 2)
-    help_products(0, 3)
-    for slot in slots:
-        hand_on(slot, 1)
-        hand_on(slot, -1)
-    help_products(3, 8)
-    for slot in slots:
-        hand_on(slot, 2)
-    help_products(8, 13)
-    early = 26
-    terms_copy = fetch(terms.at[pl.ds(0, early)], terms_out.at[pl.ds(0, early)], 4)
-    help_products(13, 16)
-    rest = terms.shape[0] - early
-    rest_copy = fetch(terms.at[pl.ds(early, rest)], terms_out.at[pl.ds(early, rest)], 5)
+    help_products(0, 4)
+    help_products(4, 8)
+    help_products(8, 12)
+    help_products(12, 14)
+    help_table.wait()
+    acc = jnp.zeros(ext.shape[1:], jnp.float32)
+    for at in range(2 * (len(HELP_ORDER) - LATE)):
+        keep = help_order[2, at].astype(jnp.float32)
+        live = help_order[1, at].astype(jnp.float32)
+        acc = acc * keep + terms[help_order[0, at]] * live
+        ext[at] = acc
+
+    @pl.loop(0, blocks)
+    def _(row):
+        sums[row] += ext[help_order[3, row]] * help_order[4, row].astype(jnp.float32)
+
+    help_products(14, 16)
+
+    @pl.loop(0, blocks)
+    def _(row):
+        acc = sums[row]
+        for k in range(len(HELP_ORDER) - LATE, len(HELP_ORDER)):
+            for slot in slots:
+                _, at, live = noted(k, slot)
+                share = (at == row).astype(jnp.float32) * live.astype(jnp.float32)
+                acc += terms[k * 2 + slot] * share
+        sums_out[row] = acc
+
     for copy in link.sent[of_ext:]:
         copy.wait_send()
-    for copy in (notes_copy, sums_copy, terms_copy, rest_copy):
-        copy.wait()
-
-
-def add_terms(notes_in, sums, terms_in, total, terms, notes, sem):
-    copies = [
-        pltpu.make_async_copy(notes_in, notes, sem.at[0]),
-        pltpu.make_async_copy(sums, total, sem.at[1]),
-        pltpu.make_async_copy(terms_in, terms, sem.at[2]),
-    ]
-    for copy in copies:
-        copy.start()
-    n = lax.axis_index("nbr")
-    x, z = n // SIDE, lax.rem(n, SIDE)
-    for copy in copies:
-        copy.wait()
-    for k, (along, across) in enumerate(HELP_ORDER):
-        for slot in (0, 1):
-            dx, dz = (along, across) if slot == 0 else (across, along)
-            source = lax.rem(x + dx, SIDE) * SIDE + lax.rem(z + dz, SIDE)
-            at = n * 2 + slot
-            row, live = notes[source, 1, 0, at], notes[source, 2, 0, at]
-            total[row] += terms[k * 2 + slot] * live.astype(jnp.float32)
 
 
 def local(sims, own_tiles, own_cols, own_rows, help_tiles, help_cols, help_rows, help_live):
@@ -521,15 +554,11 @@
     parts = (size[0], 2 * size[1])
     any_space = pl.BlockSpec(memory_space=pl.ANY)
     f32, bf16, i32 = jnp.float32, jnp.bfloat16, jnp.int32
-    sums, terms, notes = pl.pallas_call(
+    return pl.pallas_call(
         exchange,
-        out_shape=(
-            jax.ShapeDtypeStruct(sims.shape, f32),
-            jax.ShapeDtypeStruct(help_tiles.shape, f32),
-            jax.ShapeDtypeStruct((neighbours, 3, 1, helps), i32),
-        ),
+        out_shape=pltpu.VMEM(sims.shape, f32),
         in_specs=[any_space] * 8,
-        out_specs=(any_space,) * 3,
+        out_specs=pl.BlockSpec(memory_space=pltpu.VMEM),
         scratch_shapes=[
             pltpu.VMEM((extended,) + size, f32),
             pltpu.VMEM((extended,) + parts, bf16),
@@ -545,6 +574,7 @@
             pltpu.VMEM((2, 1, owns), i32),
             pltpu.VMEM((8, 256), i32),
             pltpu.SMEM((8, 256), i32),
+            pltpu.SMEM((8, 256), i32),
             pltpu.SMEM((neighbours, 3, 1, helps), i32),
             pltpu.SemaphoreType.DMA((160,)),
             pltpu.SemaphoreType.DMA((160,)),
@@ -554,7 +584,7 @@
             pltpu.SemaphoreType.DMA((2,)),
         ],
         compiler_params=pltpu.CompilerParams(
-            collective_id=0, has_side_effects=True, vmem_limit_bytes=63 * 2**20
+            collective_id=0, has_side_effects=True, vmem_limit_bytes=57 * 2**20
         ),
         name="exchange",
     )(
@@ -563,18 +593,6 @@
         own_tiles,
         *(v.reshape(1, -1) for v in (own_cols, own_rows, help_cols, help_rows, help_live)),
     )
-    return pl.pallas_call(
-        add_terms,
-        out_shape=jax.ShapeDtypeStruct(sims.shape, f32),
-        in_specs=[any_space] * 3,
-        out_specs=pl.BlockSpec(memory_space=pltpu.VMEM),
-        scratch_shapes=[
-            pltpu.VMEM(help_tiles.shape, f32),
-            pltpu.SMEM((neighbours, 3, 1, helps), i32),
-            pltpu.SemaphoreType.DMA((3,)),
-        ],
-        name="add_terms",
-    )(notes, sums, terms)
 
 
 def solution(mesh):

time: 127 us -> 120 us (0.945)
  Pallas kernels: 126 us -> 118 us
    pallas_call x2 -> x1, Pallas kernels: 126 us -> 118 us  [local(): pl.pallas_call(exchange, out_shape=pltpu.VMEM(sims.shape, f32), in_specs=...]
where the time goes in v3:
time: 120 us; the launch traced here: 119 us
  Pallas kernels  118 us (98%)
    pallas_call x1, Pallas kernels, local(): pl.pallas_call(exchange, out_shape=pltpu.VMEM(sims.shape, f32), in_specs=...  118 us

profile of v3, /device:TPU:1, one launch (start us, length us, event | category | flops | bytes accessed | tf_op | source)
XLA Modules:
  0.0 119.0 jit_solution(1754373001960216954)
XLA Ops:
  0.0 118.0 %exchange.1 = f32[16,128,128]{2,1,0:T(8,128)S(1)} custom-call(f32[16,128,128]{2,1,0:T(8,128)} %sims.1, f32[4,4,2,128,128]{4,3,2,1,0:T(8,128)} %bitcast.6, f32[192,128,128]{2,1,0:T(8,128)} %tiles.1, s32[1,192]{1,0:T(1,128)} %bitcast.7, s32[1,192]{1,0:T(1,128)} %bitcast.8, s32[1,32]{1,0:T(1,128)} %bitcast.9, s32[1,32]{1,0:T(1,128)} %bitcast.10, s32[1,32]{1,0:T(1,128)} %bitcast.11), custom_call_target="tpu_custom_call" | custom-call | tf_op jit(solution)/shard_map/exchange/pallas_call | solution.py:557
  118.0 1.0 copy.10

commit v4 on v3

--- a/solution.py
+++ b/solution.py
@@ -127,7 +127,7 @@
     sims, helps, tiles, own_cols, own_rows, help_cols, help_rows, help_live,
     sums_out,
     ext, ext_parts, tile_parts, stage, first, passing, second, arrived, terms, sums,
-    metas, vec, table, order, help_order, notes,
+    metas, vec, table, order, help_order, late_order, notes,
     send, recv, rim_send, rim_recv, local_sem, stage_sem,
 ):
     n, g = lax.axis_index("nbr"), lax.axis_index("grp")
@@ -165,30 +165,15 @@
         copy.start()
         return copy
 
-    mine = fetch(sims, ext.at[pl.ds(RIM + n * blocks, blocks)], 0)
-    told = [
-        fetch(ref, metas.at[n, k], 1 + k) for k, ref in enumerate((help_cols, help_rows, help_live))
-    ]
-    bundles = [
-        fetch(helps.at[x, :, 0], first.at[0, 0], 4), fetch(helps.at[:, z, 1], first.at[1, 0], 5)
-    ]
-    vectors = [fetch(own_cols, vec.at[0], 6), fetch(own_rows, vec.at[1], 7)]
-
     def load(chunk):
         at = lax.rem(chunk, 2)
         return pltpu.make_async_copy(
             tiles.at[pl.ds(chunk * UNIT, UNIT)], stage.at[at], stage_sem.at[at]
         )
 
-    for chunk in (0, 1):
-        load(chunk).start()
-
     pl.semaphore_wait(
         barrier, 4 + (g > 0).astype(jnp.int32) + (g < groups - 1).astype(jnp.int32)
     )
-    mine.wait()
-    for copy in told:
-        copy.wait()
     link = Link(send, recv)
 
     def split_unit(start):
@@ -244,7 +229,7 @@
             return
         here.add(name)
         fresh.append((origin, sub))
-        if name >= 4:
+        if wrap(origin[0]) or wrap(origin[1]):
             link.arrive(quarter(origin, sub), name, neighbour(0, 1))
 
     def tidy():
@@ -257,7 +242,10 @@
     base = 64
 
     def note_row(dx):
-        return metas.at[lax.rem(x + dx + SIDE, SIDE) * SIDE + z]
+        return metas.at[lax.rem(x + dx + SIDE, SIDE), z]
+
+    def note_column(dz):
+        return metas.at[:, lax.rem(z + dz + SIDE, SIDE)]
 
     def note_wait(ref, arrival):
         link.arrive(ref, arrival, neighbour(0, 1))
@@ -335,6 +323,7 @@
         note_wait(first.at[slot, -way % SIDE], arrival(slot, 2 + k))
 
     slots = (0, 1)
+    early = len(HELP_ORDER) - LATE
 
     def rim(has, pieces, start):
         @pl.when(has)
@@ -350,65 +339,82 @@
 
     def noted(k, slot):
         along, across = HELP_ORDER[k]
-        source = place((along, across) if slot == 0 else (across, along))
-        return [notes[source, kind, 0, n * 2 + slot] for kind in range(3)]
-
-    def list_rows():
+        dx, dz = (along, across) if slot == 0 else (across, along)
+        sx, sz = lax.rem(x + dx, SIDE), lax.rem(z + dz, SIDE)
+        return [notes[sx, sz, kind, 0, n * 2 + slot] for kind in range(3)]
+
+    def list_rows(low, high, lines, k):
         spots = lax.broadcasted_iota(jnp.int32, (1, terms.shape[0]), 1)
-        help_rows_line = jnp.full_like(spots, blocks)
-        help_live_line = jnp.zeros_like(spots)
-        for k in range(len(HELP_ORDER) - LATE):
+        rows, load = jnp.full_like(spots, blocks), jnp.zeros_like(spots)
+        for each in range(low, high):
             for slot in slots:
-                _, row, live = noted(k, slot)
-                help_rows_line = jnp.where(spots == k * 2 + slot, row, help_rows_line)
-                help_live_line = jnp.where(spots == k * 2 + slot, live, help_live_line)
-        order_table(help_live_line, help_rows_line, table)
-        help_table = fetch(table, help_order, 2)
-        return help_table
+                col, row, live = noted(each, slot)
+                here = spots == (each - low) * 2 + slot
+                rows = jnp.where(here, row, rows)
+                load = jnp.where(here, col * 2 + live, load)
+        order_table(load, rows, table)
+        return fetch(table, lines, k)
 
     queues = gather_queues()
     turns = len(queues[0][2])
-    chunks = n_own // UNIT
     for turn in range(turns):
         for axis, way, queue, _ in queues:
             origin, sub = queue[turn]
             need(origin, sub)
             seen = (origin[0] - step(axis, way)[0], origin[1] - step(axis, way)[1])
             link.start(
-                quarter(origin, sub), quarter(origin, sub), unit_id(seen, sub), neighbour(axis, way)
+                quarter(origin, sub) if any(origin) else sims.at[pl.ds(sub * UNIT, UNIT)],
+                quarter(origin, sub),
+                unit_id(seen, sub),
+                neighbour(axis, way),
             )
         if turn == 0:
+            mine = fetch(sims, ext.at[pl.ds(RIM + n * blocks, blocks)], 0)
+            told = [
+                fetch(ref, metas.at[x, z, k], 1 + k)
+                for k, ref in enumerate((help_cols, help_rows, help_live))
+            ]
+            vectors = [fetch(own_cols, vec.at[0], 6), fetch(own_rows, vec.at[1], 7)]
+            for chunk in (0, 1):
+                load(chunk).start()
+            bundles = [
+                fetch(helps.at[x, :, 0], first.at[0, 0], 4),
+                fetch(helps.at[:, z, 1], first.at[1, 0], 5),
+            ]
+        if turn == 2:
+            for copy in told:
+                copy.wait()
             link.start(note_row(0), note_row(0), base, neighbour(0, 1))
             link.start(note_row(0), note_row(0), base + 1, neighbour(0, -1))
-        if turn == 3:
+            mine.wait()
+        if turn == 4:
             note_wait(note_row(-1), base)
             note_wait(note_row(1), base + 1)
             link.start(note_row(-1), note_row(-1), base + 2, neighbour(0, 1))
-        if turn == 6:
+        if turn == 7:
             note_wait(note_row(2), base + 2)
-            for dx in range(SIDE):
-                link.start(note_row(dx), note_row(dx), base + 3 + dx, neighbour(1, 1))
-                link.start(note_row(dx), note_row(dx), base + 7 + dx, neighbour(1, -1))
-        if turn == 9:
-            for dx in range(SIDE):
-                behind = metas.at[place((dx, -1))]
-                note_wait(behind, base + 3 + dx)
-                note_wait(metas.at[place((dx, 1))], base + 7 + dx)
-                link.start(behind, behind, base + 11 + dx, neighbour(1, 1))
+            link.start(note_column(0), note_column(0), base + 3, neighbour(1, 1))
+            link.start(note_column(0), note_column(0), base + 4, neighbour(1, -1))
         for slot in slots:
-            if turn == 5:
+            if turn == 3:
                 far_pairs(slot)
+            if turn == 6:
+                relay(slot)
             if turn == 8:
-                relay(slot)
-            if turn == turns - 1:
                 bundle(slot)
+        if turn < 2:
+            continue
         tidy()
-        if turn == 1:
+        if turn == 2:
             for copy in vectors:
                 copy.wait()
             order_table(vec[0], vec[1], table)
             fetch(table, order, 6).wait()
-        split_tiles(chunks * turn // turns, chunks * (turn + 1) // turns)
+        chunks, spread = n_own // UNIT, turns - 2
+        split_tiles(chunks * (turn - 2) // spread, chunks * (turn - 1) // spread)
+    note_wait(note_column(-1), base + 3)
+    note_wait(note_column(1), base + 4)
+    link.start(note_column(-1), note_column(-1), base + 5, neighbour(1, 1))
 
     for axis, way, _, sub in queues:
         for across in range(SIDE):
@@ -447,8 +453,8 @@
     for along in (0, 1, 3, 2):
         for slot in slots:
             direct(slot, along)
-    for dx in range(SIDE):
-        note_wait(metas.at[place((dx, 2))], base + 11 + dx)
+    late = len(link.sent)
+    note_wait(note_column(2), base + 5)
     fetch(metas, notes, 1).wait()
 
     for k in range(SIDE):
@@ -459,7 +465,10 @@
             fresh.append((origin, sub))
         tidy()
         if k == 0:
-            help_table = list_rows()
+            help_table = list_rows(0, early, help_order, 2)
+        if k == 1:
+            help_table.wait()
+            late_table = list_rows(early, len(HELP_ORDER), late_order, 3)
     rim(g > 0, (0, 1), 0)
     rim(g < groups - 1, (2, 3), total - RIM)
     for copy in link.sent[:of_ext]:
@@ -517,12 +526,11 @@
     help_products(0, 4)
     help_products(4, 8)
     help_products(8, 12)
-    help_products(12, 14)
-    help_table.wait()
+    help_products(12, early)
     acc = jnp.zeros(ext.shape[1:], jnp.float32)
-    for at in range(2 * (len(HELP_ORDER) - LATE)):
+    for at in range(2 * early):
         keep = help_order[2, at].astype(jnp.float32)
-        live = help_order[1, at].astype(jnp.float32)
+        live = jnp.bitwise_and(help_order[1, at], 1).astype(jnp.float32)
         acc = acc * keep + terms[help_order[0, at]] * live
         ext[at] = acc
 
@@ -530,19 +538,26 @@
     def _(row):
         sums[row] += ext[help_order[3, row]] * help_order[4, row].astype(jnp.float32)
 
-    help_products(14, 16)
+    late_table.wait()
+    for copy in link.sent[of_ext:late]:
+        copy.wait_send()
+    for along, across in HELP_ORDER[early:]:
+        for slot in slots:
+            note_wait(final(slot, along, across), arrival(slot, 6 + along * 4 + across))
+    acc = jnp.zeros(ext.shape[1:], jnp.float32)
+    for at in range(2 * LATE):
+        which, load = late_order[0, at], late_order[1, at]
+        tile = arrived[lax.rem(which, 2), 1 + which // 2, 1]
+        keep = late_order[2, at].astype(jnp.float32)
+        live = jnp.bitwise_and(load, 1).astype(jnp.float32)
+        acc = acc * keep + product(split(tile), ext_parts[jnp.right_shift(load, 1)]) * live
+        ext[at] = acc
 
     @pl.loop(0, blocks)
     def _(row):
-        acc = sums[row]
-        for k in range(len(HELP_ORDER) - LATE, len(HELP_ORDER)):
-            for slot in slots:
-                _, at, live = noted(k, slot)
-                share = (at == row).astype(jnp.float32) * live.astype(jnp.float32)
-                acc += terms[k * 2 + slot] * share
-        sums_out[row] = acc
-
-    for copy in link.sent[of_ext:]:
+        sums_out[row] = sums[row] + ext[late_order[3, row]] * late_order[4, row].astype(jnp.float32)
+
+    for copy in link.sent[late:]:
         copy.wait_send()
 
 
@@ -570,12 +585,13 @@
             pltpu.VMEM((2, SIDE, SIDE - 1) + size, f32),
             pltpu.VMEM((helps,) + size, f32),
             pltpu.VMEM(sims.shape, f32),
-            pltpu.VMEM((neighbours, 3, 1, helps), i32),
+            pltpu.VMEM((SIDE, SIDE, 3, 1, helps), i32),
             pltpu.VMEM((2, 1, owns), i32),
             pltpu.VMEM((8, 256), i32),
             pltpu.SMEM((8, 256), i32),
             pltpu.SMEM((8, 256), i32),
-            pltpu.SMEM((neighbours, 3, 1, helps), i32),
+            pltpu.SMEM((8, 256), i32),
+            pltpu.SMEM((SIDE, SIDE, 3, 1, helps), i32),
             pltpu.SemaphoreType.DMA((160,)),
             pltpu.SemaphoreType.DMA((160,)),
             pltpu.SemaphoreType.DMA((4,)),

time: 120 us -> 120 us (level)
  no operation moved by 1% of the time
where the time goes in v4:
time: 120 us; the launch traced here: 119 us
  Pallas kernels  118 us (98%)
    pallas_call x1, Pallas kernels, local(): pl.pallas_call(exchange, out_shape=pltpu.VMEM(sims.shape, f32), in_specs=...  118 us

profile of v4, /device:TPU:1, one launch (start us, length us, event | category | flops | bytes accessed | tf_op | source)
XLA Modules:
  0.0 118.9 jit_solution(14474271811390322693)
XLA Ops:
  0.0 117.9 %exchange.1 = f32[16,128,128]{2,1,0:T(8,128)S(1)} custom-call(f32[16,128,128]{2,1,0:T(8,128)} %sims.1, f32[4,4,2,128,128]{4,3,2,1,0:T(8,128)} %bitcast.6, f32[192,128,128]{2,1,0:T(8,128)} %tiles.1, s32[1,192]{1,0:T(1,128)} %bitcast.7, s32[1,192]{1,0:T(1,128)} %bitcast.8, s32[1,32]{1,0:T(1,128)} %bitcast.9, s32[1,32]{1,0:T(1,128)} %bitcast.10, s32[1,32]{1,0:T(1,128)} %bitcast.11), custom_call_target="tpu_custom_call" | custom-call | tf_op jit(solution)/shard_map/exchange/pallas_call | solution.py:572
  117.9 1.0 copy.10

commit v5 on v4

--- a/solution.py
+++ b/solution.py
@@ -10,14 +10,11 @@
 SIDE = 4
 UNROLL = 16
 MESH = pl.DeviceIdType.MESH
+GATHER, HELPER, NOTES = 0, 1, 2
 
 
 def wrap(value):
     return (value + SIDE) % SIDE if isinstance(value, int) else lax.rem(value + SIDE, SIDE)
-
-
-def unit_id(origin, sub):
-    return (wrap(origin[0]) * SIDE + wrap(origin[1])) * 4 + sub
 
 
 def gather_queues():
@@ -50,29 +47,27 @@
 
 class Link:
     def __init__(self, send, recv):
-        self.send, self.recv, self.sent = send, recv, []
-
-    def start(self, src, dst, arrival, device):
-        copy = pltpu.make_async_remote_copy(
+        self.send, self.recv = send, recv
+
+    def start(self, src, dst, sent, arrival, device):
+        pltpu.make_async_remote_copy(
             src_ref=src,
             dst_ref=dst,
-            send_sem=self.send.at[len(self.sent)],
+            send_sem=self.send.at[sent],
+            recv_sem=self.recv.at[arrival],
+            device_id=device,
+            device_id_type=MESH,
+        ).start()
+
+    def whole(self, ref, sent, arrival, device):
+        return pltpu.make_async_remote_copy(
+            src_ref=ref,
+            dst_ref=ref,
+            send_sem=self.send.at[sent],
             recv_sem=self.recv.at[arrival],
             device_id=device,
             device_id_type=MESH,
         )
-        copy.start()
-        self.sent.append(copy)
-
-    def arrive(self, dst, arrival, device):
-        pltpu.make_async_remote_copy(
-            src_ref=dst,
-            dst_ref=dst,
-            send_sem=self.send.at[0],
-            recv_sem=self.recv.at[arrival],
-            device_id=device,
-            device_id_type=MESH,
-        ).wait_recv()
 
 
 def split(value):
@@ -137,6 +132,7 @@
     total = ext.shape[0]
     n_own = tiles.shape[0]
     last = SIDE * SIDE - 1
+    helps_dev = terms.shape[0]
 
     def place(origin):
         return lax.rem(x + origin[0] + SIDE, SIDE) * SIDE + lax.rem(z + origin[1] + SIDE, SIDE)
@@ -220,17 +216,26 @@
     def quarter(origin, sub):
         return ext.at[pl.ds(base_of(origin, sub), UNIT)]
 
+    queues = gather_queues()
+    turns = len(queues[0][2])
+    groups_of = {}
+    for axis, way, queue, _ in queues:
+        for turn, (origin, sub) in enumerate(queue):
+            dx, dz = step(axis, way)
+            groups_of[wrap(origin[0] - dx), wrap(origin[1] - dz), sub] = turn
     here = set()
-    fresh = []
+    fresh = [((0, 0), sub) for sub in range(4)]
+
+    def arrive(ref, arrival):
+        link.whole(ref, 0, arrival, neighbour(0, 1)).wait_recv()
 
     def need(origin, sub):
-        name = unit_id(origin, sub)
-        if name in here:
+        turn = groups_of.get((wrap(origin[0]), wrap(origin[1]), sub))
+        if turn is None or turn in here:
             return
-        here.add(name)
-        fresh.append((origin, sub))
-        if wrap(origin[0]) or wrap(origin[1]):
-            link.arrive(quarter(origin, sub), name, neighbour(0, 1))
+        here.add(turn)
+        fresh.extend(((a, b), each) for (a, b, each), when in groups_of.items() if when == turn)
+        arrive(ext.at[pl.ds(0, len(queues) * UNIT)], turn)
 
     def tidy():
         for origin, sub in fresh:
@@ -239,7 +244,7 @@
             split_unit(base_of(origin, sub))
         fresh.clear()
 
-    base = 64
+    base = turns + SIDE
 
     def note_row(dx):
         return metas.at[lax.rem(x + dx + SIDE, SIDE), z]
@@ -247,8 +252,8 @@
     def note_column(dz):
         return metas.at[:, lax.rem(z + dz + SIDE, SIDE)]
 
-    def note_wait(ref, arrival):
-        link.arrive(ref, arrival, neighbour(0, 1))
+    def note_wait(ref, k):
+        arrive(ref, base + k)
 
     def bundle_of(slot, to):
         at = place(to)
@@ -262,8 +267,7 @@
     def final(slot, along, across):
         return arrived.at[slot, along % SIDE, across % SIDE - 1]
 
-    def arrival(slot, kind):
-        return 79 + slot * 28 + kind
+    passed, begun, turned, ended = base + 6, base + 7, base + 8, base + 10
 
     def target(slot, way):
         axis = 1 - slot
@@ -272,55 +276,46 @@
 
     def far_pairs(slot):
         for way, low in ((1, 0), (-1, 2)):
-            k = 0 if way > 0 else 1
             link.start(
-                pair_of(slot, step(slot, 2), low), passing.at[slot, k], arrival(slot, k),
-                neighbour(slot, way),
+                pair_of(slot, step(slot, 2), low), passing.at[slot, 0 if way > 0 else 1],
+                HELPER, passed, neighbour(slot, way),
             )
 
     def bundle(slot):
         for way in (1, -1):
             link.start(
                 bundle_of(slot, step(slot, way)), first.at[slot, -way % SIDE],
-                arrival(slot, 2 + (0 if way > 0 else 1)), neighbour(slot, way),
+                HELPER, begun, neighbour(slot, way),
             )
 
     def relay(slot):
         for way, low in ((1, 0), (-1, 2)):
-            k = 0 if way > 0 else 1
-            note_wait(passing.at[slot, k], arrival(slot, k))
             link.start(
-                passing.at[slot, k], first.at[slot, 2, pl.ds(low, 2)], arrival(slot, 4 + k),
-                neighbour(slot, way),
+                passing.at[slot, 0 if way > 0 else 1], first.at[slot, 2, pl.ds(low, 2)],
+                HELPER, begun, neighbour(slot, way),
             )
 
     def direct(slot, along):
         for way in (1, -1):
             link.start(
-                first.at[slot, along % SIDE, target(slot, way)], final(slot, along, -way),
-                arrival(slot, 6 + (along % SIDE) * 4 + (-way) % SIDE), neighbour(1 - slot, way),
+                first.at[slot, along, target(slot, way)], final(slot, along, -way),
+                HELPER, ended + along // 2, neighbour(1 - slot, way),
             )
 
     by = {0: 1, 1: 1, 3: -1, 2: -1}
+    soon = (0, 3)
 
     def detour(slot, along):
-        way = by[along % SIDE]
         link.start(
-            first.at[slot, along % SIDE, target(slot, 2)], second.at[slot, along % SIDE],
-            arrival(slot, 22 + along % SIDE), neighbour(1 - slot, way),
+            first.at[slot, along, target(slot, 2)], second.at[slot, along],
+            HELPER, turned + (0 if along in soon else 1), neighbour(1 - slot, by[along]),
         )
 
     def hand_on(slot, along):
-        way = by[along % SIDE]
-        note_wait(second.at[slot, along % SIDE], arrival(slot, 22 + along % SIDE))
         link.start(
-            second.at[slot, along % SIDE], final(slot, along, 2),
-            arrival(slot, 6 + (along % SIDE) * 4 + 2), neighbour(1 - slot, way),
+            second.at[slot, along], final(slot, along, 2),
+            HELPER, ended + (2 if along in soon else 3), neighbour(1 - slot, by[along]),
         )
-
-    def bundle_wait(slot, way):
-        k = 0 if way > 0 else 1
-        note_wait(first.at[slot, -way % SIDE], arrival(slot, 2 + k))
 
     slots = (0, 1)
     early = len(HELP_ORDER) - LATE
@@ -355,17 +350,15 @@
         order_table(load, rows, table)
         return fetch(table, lines, k)
 
-    queues = gather_queues()
-    turns = len(queues[0][2])
     for turn in range(turns):
         for axis, way, queue, _ in queues:
             origin, sub = queue[turn]
             need(origin, sub)
-            seen = (origin[0] - step(axis, way)[0], origin[1] - step(axis, way)[1])
             link.start(
                 quarter(origin, sub) if any(origin) else sims.at[pl.ds(sub * UNIT, UNIT)],
                 quarter(origin, sub),
-                unit_id(seen, sub),
+                GATHER,
+                turn,
                 neighbour(axis, way),
             )
         if turn == 0:
@@ -384,21 +377,23 @@
         if turn == 2:
             for copy in told:
                 copy.wait()
-            link.start(note_row(0), note_row(0), base, neighbour(0, 1))
-            link.start(note_row(0), note_row(0), base + 1, neighbour(0, -1))
+            link.start(note_row(0), note_row(0), NOTES + 0, base + 0, neighbour(0, 1))
+            link.start(note_row(0), note_row(0), NOTES + 1, base + 1, neighbour(0, -1))
             mine.wait()
         if turn == 4:
-            note_wait(note_row(-1), base)
-            note_wait(note_row(1), base + 1)
-            link.start(note_row(-1), note_row(-1), base + 2, neighbour(0, 1))
+            note_wait(note_row(-1), 0)
+            note_wait(note_row(1), 1)
+            link.start(note_row(-1), note_row(-1), NOTES + 2, base + 2, neighbour(0, 1))
         if turn == 7:
-            note_wait(note_row(2), base + 2)
-            link.start(note_column(0), note_column(0), base + 3, neighbour(1, 1))
-            link.start(note_column(0), note_column(0), base + 4, neighbour(1, -1))
+            note_wait(note_row(2), 2)
+            link.start(note_column(0), note_column(0), NOTES + 3, base + 3, neighbour(1, 1))
+            link.start(note_column(0), note_column(0), NOTES + 4, base + 4, neighbour(1, -1))
         for slot in slots:
             if turn == 3:
                 far_pairs(slot)
             if turn == 6:
+                if slot == 0:
+                    arrive(passing, passed)
                 relay(slot)
             if turn == 8:
                 bundle(slot)
@@ -412,9 +407,9 @@
             fetch(table, order, 6).wait()
         chunks, spread = n_own // UNIT, turns - 2
         split_tiles(chunks * (turn - 2) // spread, chunks * (turn - 1) // spread)
-    note_wait(note_column(-1), base + 3)
-    note_wait(note_column(1), base + 4)
-    link.start(note_column(-1), note_column(-1), base + 5, neighbour(1, 1))
+    note_wait(note_column(-1), 3)
+    note_wait(note_column(1), 4)
+    link.start(note_column(-1), note_column(-1), NOTES + 5, base + 5, neighbour(1, 1))
 
     for axis, way, _, sub in queues:
         for across in range(SIDE):
@@ -428,11 +423,9 @@
         for axis, way, _, sub in queues:
             across = ahead(axis, k)
             origin = (-way, across) if axis == 0 else (across, -way)
-            seen = (-2, across) if axis == 0 else (across, -2)
             link.start(
-                quarter(origin, sub), quarter(origin, sub), unit_id(seen, sub), neighbour(axis, way)
+                quarter(origin, sub), quarter(origin, sub), GATHER, turns + k, neighbour(axis, way)
             )
-    of_ext = len(link.sent)
     for a in range(SIDE):
         for b in range(SIDE):
             for sub in range(4):
@@ -442,27 +435,22 @@
     for copy in bundles:
         copy.wait()
 
-    for slot in slots:
-        for k, low in ((0, 0), (1, 2)):
-            note_wait(first.at[slot, 2, pl.ds(low, 2)], arrival(slot, 4 + k))
-        for way in (1, -1):
-            bundle_wait(slot, way)
+    arrive(first.at[:, pl.ds(1, SIDE - 1)], begun)
     for along in (0, 3, 1, 2):
         for slot in slots:
             detour(slot, along)
     for along in (0, 1, 3, 2):
         for slot in slots:
             direct(slot, along)
-    late = len(link.sent)
-    note_wait(note_column(2), base + 5)
+    note_wait(note_column(2), 5)
     fetch(metas, notes, 1).wait()
 
     for k in range(SIDE):
         for axis, way, _, sub in queues:
             across = ahead(axis, k)
             origin = (2, across) if axis == 0 else (across, 2)
-            link.arrive(quarter(origin, sub), unit_id(origin, sub), neighbour(0, 1))
             fresh.append((origin, sub))
+        arrive(ext.at[pl.ds(0, len(queues) * UNIT)], turns + k)
         tidy()
         if k == 0:
             help_table = list_rows(0, early, help_order, 2)
@@ -471,8 +459,7 @@
             late_table = list_rows(early, len(HELP_ORDER), late_order, 3)
     rim(g > 0, (0, 1), 0)
     rim(g < groups - 1, (2, 3), total - RIM)
-    for copy in link.sent[:of_ext]:
-        copy.wait_send()
+    link.whole(ext.at[pl.ds(0, len(queues) * (turns + SIDE) * UNIT)], GATHER, 0, neighbour(0, 1)).wait_send()
 
     @pl.when(g < groups - 1)
     def _():
@@ -497,11 +484,6 @@
         lax.fori_loop(0, (high - low) // UNROLL, body, acc)
 
     def help_products(low, high):
-        for k in range(low, high):
-            along, across = HELP_ORDER[k]
-            for slot in slots:
-                if across:
-                    note_wait(final(slot, along, across), arrival(slot, 6 + along * 4 + across))
         for k in range(low, high):
             along, across = HELP_ORDER[k]
             for slot in slots:
@@ -514,9 +496,11 @@
 
     cut = n_own // 2
     own(0, cut)
-    for along in (0, 3, 1, 2):
-        for slot in slots:
-            hand_on(slot, along)
+    for k, part in enumerate((soon, (1, 2))):
+        arrive(second.at[0], turned + k)
+        for along in part:
+            for slot in slots:
+                hand_on(slot, along)
     own(cut, n_own)
 
     @pl.loop(0, blocks)
@@ -524,8 +508,11 @@
         sums[row] = ext[order[3, row]] * order[4, row].astype(jnp.float32)
 
     help_products(0, 4)
+    arrive(first.at[0, pl.ds(0, 2)], ended)
     help_products(4, 8)
+    arrive(first.at[0, pl.ds(0, 2)], ended + 1)
     help_products(8, 12)
+    arrive(second.at[0], ended + 2)
     help_products(12, early)
     acc = jnp.zeros(ext.shape[1:], jnp.float32)
     for at in range(2 * early):
@@ -539,11 +526,10 @@
         sums[row] += ext[help_order[3, row]] * help_order[4, row].astype(jnp.float32)
 
     late_table.wait()
-    for copy in link.sent[of_ext:late]:
-        copy.wait_send()
-    for along, across in HELP_ORDER[early:]:
-        for slot in slots:
-            note_wait(final(slot, along, across), arrival(slot, 6 + along * 4 + across))
+    for k in range(3):
+        link.whole(note_row(0), NOTES + k, 0, neighbour(0, 1)).wait_send()
+        link.whole(note_column(0), NOTES + 3 + k, 0, neighbour(0, 1)).wait_send()
+    arrive(second.at[0], ended + 3)
     acc = jnp.zeros(ext.shape[1:], jnp.float32)
     for at in range(2 * LATE):
         which, load = late_order[0, at], late_order[1, at]
@@ -557,8 +543,7 @@
     def _(row):
         sums_out[row] = sums[row] + ext[late_order[3, row]] * late_order[4, row].astype(jnp.float32)
 
-    for copy in link.sent[late:]:
-        copy.wait_send()
+    link.whole(ext.at[pl.ds(0, 2 * helps_dev)], HELPER, 0, neighbour(0, 1)).wait_send()
 
 
 def local(sims, own_tiles, own_cols, own_rows, help_tiles, help_cols, help_rows, help_live):
@@ -592,8 +577,8 @@
             pltpu.SMEM((8, 256), i32),
             pltpu.SMEM((8, 256), i32),
             pltpu.SMEM((SIDE, SIDE, 3, 1, helps), i32),
-            pltpu.SemaphoreType.DMA((160,)),
-            pltpu.SemaphoreType.DMA((160,)),
+            pltpu.SemaphoreType.DMA((8,)),
+            pltpu.SemaphoreType.DMA((29,)),
             pltpu.SemaphoreType.DMA((4,)),
             pltpu.SemaphoreType.DMA((4,)),
             pltpu.SemaphoreType.DMA((8,)),

time: 120 us -> 117 us (0.975)
  Pallas kernels: 118 us -> 115 us
    pallas_call x1, Pallas kernels: 118 us -> 115 us  [local(): pl.pallas_call(exchange, out_shape=pltpu.VMEM(sims.shape, f32), in_specs=...]
where the time goes in v5:
time: 117 us; the launch traced here: 116 us
  Pallas kernels  115 us (98%)
    pallas_call x1, Pallas kernels, local(): pl.pallas_call(exchange, out_shape=pltpu.VMEM(sims.shape, f32), in_specs=...  115 us

profile of v5, /device:TPU:1, one launch (start us, length us, event | category | flops | bytes accessed | tf_op | source)
XLA Modules:
  0.0 116.3 jit_solution(11525917385024593768)
XLA Ops:
  0.0 115.3 %exchange.1 = f32[16,128,128]{2,1,0:T(8,128)S(1)} custom-call(f32[16,128,128]{2,1,0:T(8,128)} %sims.1, f32[4,4,2,128,128]{4,3,2,1,0:T(8,128)} %bitcast.6, f32[192,128,128]{2,1,0:T(8,128)} %tiles.1, s32[1,192]{1,0:T(1,128)} %bitcast.7, s32[1,192]{1,0:T(1,128)} %bitcast.8, s32[1,32]{1,0:T(1,128)} %bitcast.9, s32[1,32]{1,0:T(1,128)} %bitcast.10, s32[1,32]{1,0:T(1,128)} %bitcast.11), custom_call_target="tpu_custom_call" | custom-call | tf_op jit(solution)/shard_map/exchange/pallas_call | solution.py:557
  115.3 1.0 copy.10

commit v6 on v5

--- a/solution.py
+++ b/solution.py
@@ -198,8 +198,16 @@
         peer = lax.rem(g + 1, groups) if up else lax.rem(g + groups - 1, groups)
         return pltpu.make_async_remote_copy(
             src_ref=ext.at[pl.ds(src, UNIT)], dst_ref=ext.at[pl.ds(dst, UNIT)],
-            send_sem=rim_send.at[piece], recv_sem=rim_recv.at[piece],
+            send_sem=rim_send.at[piece // 2], recv_sem=rim_recv.at[piece // 2],
             device_id={"grp": peer}, device_id_type=MESH,
+        )
+
+    def rim_whole(up):
+        ref = ext.at[pl.ds(0 if up else total - RIM, RIM)]
+        return pltpu.make_async_remote_copy(
+            src_ref=ref, dst_ref=ref,
+            send_sem=rim_send.at[0 if up else 1], recv_sem=rim_recv.at[0 if up else 1],
+            device_id=neighbour(0, 1), device_id_type=MESH,
         )
 
     def rim_leaves(origin, sub):
@@ -267,7 +275,7 @@
     def final(slot, along, across):
         return arrived.at[slot, along % SIDE, across % SIDE - 1]
 
-    passed, begun, turned, ended = base + 6, base + 7, base + 8, base + 10
+    passed, begun, turned, ended = base + 6, base + 7, base + 8, base + 9
 
     def target(slot, way):
         axis = 1 - slot
@@ -295,20 +303,21 @@
                 HELPER, begun, neighbour(slot, way),
             )
 
-    def direct(slot, along):
+    def direct(slot, low):
         for way in (1, -1):
             link.start(
-                first.at[slot, along, target(slot, way)], final(slot, along, -way),
-                HELPER, ended + along // 2, neighbour(1 - slot, way),
+                first.at[slot, pl.ds(low, 2), target(slot, way)],
+                arrived.at[slot, pl.ds(low, 2), -way % SIDE - 1],
+                HELPER, ended + low // 2, neighbour(1 - slot, way),
             )
 
     by = {0: 1, 1: 1, 3: -1, 2: -1}
     soon = (0, 3)
 
-    def detour(slot, along):
+    def detour(slot, low):
         link.start(
-            first.at[slot, along, target(slot, 2)], second.at[slot, along],
-            HELPER, turned + (0 if along in soon else 1), neighbour(1 - slot, by[along]),
+            first.at[slot, pl.ds(low, 2), target(slot, 2)], second.at[slot, pl.ds(low, 2)],
+            HELPER, turned, neighbour(1 - slot, by[low]),
         )
 
     def hand_on(slot, along):
@@ -320,11 +329,10 @@
     slots = (0, 1)
     early = len(HELP_ORDER) - LATE
 
-    def rim(has, pieces, start):
+    def rim(has, start):
         @pl.when(has)
         def _():
-            for piece in pieces:
-                rim_copy(piece).wait_recv()
+            rim_whole(start == 0).wait_recv()
             for k in range(RIM // UNIT):
                 split_unit(start + k * UNIT)
 
@@ -377,17 +385,17 @@
         if turn == 2:
             for copy in told:
                 copy.wait()
-            link.start(note_row(0), note_row(0), NOTES + 0, base + 0, neighbour(0, 1))
-            link.start(note_row(0), note_row(0), NOTES + 1, base + 1, neighbour(0, -1))
+            link.start(note_row(0), note_row(0), NOTES, base + 0, neighbour(0, 1))
+            link.start(note_row(0), note_row(0), NOTES, base + 1, neighbour(0, -1))
             mine.wait()
         if turn == 4:
             note_wait(note_row(-1), 0)
             note_wait(note_row(1), 1)
-            link.start(note_row(-1), note_row(-1), NOTES + 2, base + 2, neighbour(0, 1))
+            link.start(note_row(-1), note_row(-1), NOTES, base + 2, neighbour(0, 1))
         if turn == 7:
             note_wait(note_row(2), 2)
-            link.start(note_column(0), note_column(0), NOTES + 3, base + 3, neighbour(1, 1))
-            link.start(note_column(0), note_column(0), NOTES + 4, base + 4, neighbour(1, -1))
+            link.start(note_column(0), note_column(0), NOTES + 1, base + 3, neighbour(1, 1))
+            link.start(note_column(0), note_column(0), NOTES + 1, base + 4, neighbour(1, -1))
         for slot in slots:
             if turn == 3:
                 far_pairs(slot)
@@ -409,7 +417,7 @@
         split_tiles(chunks * (turn - 2) // spread, chunks * (turn - 1) // spread)
     note_wait(note_column(-1), 3)
     note_wait(note_column(1), 4)
-    link.start(note_column(-1), note_column(-1), NOTES + 5, base + 5, neighbour(1, 1))
+    link.start(note_column(-1), note_column(-1), NOTES + 1, base + 5, neighbour(1, 1))
 
     for axis, way, _, sub in queues:
         for across in range(SIDE):
@@ -436,12 +444,12 @@
         copy.wait()
 
     arrive(first.at[:, pl.ds(1, SIDE - 1)], begun)
-    for along in (0, 3, 1, 2):
+    for low in (0, 2):
         for slot in slots:
-            detour(slot, along)
-    for along in (0, 1, 3, 2):
+            detour(slot, low)
+    for low in (0, 2):
         for slot in slots:
-            direct(slot, along)
+            direct(slot, low)
     note_wait(note_column(2), 5)
     fetch(metas, notes, 1).wait()
 
@@ -457,19 +465,17 @@
         if k == 1:
             help_table.wait()
             late_table = list_rows(early, len(HELP_ORDER), late_order, 3)
-    rim(g > 0, (0, 1), 0)
-    rim(g < groups - 1, (2, 3), total - RIM)
+    rim(g > 0, 0)
+    rim(g < groups - 1, total - RIM)
     link.whole(ext.at[pl.ds(0, len(queues) * (turns + SIDE) * UNIT)], GATHER, 0, neighbour(0, 1)).wait_send()
 
     @pl.when(g < groups - 1)
     def _():
-        for piece in (0, 1):
-            rim_copy(piece).wait_send()
+        rim_whole(True).wait_send()
 
     @pl.when(g > 0)
     def _():
-        for piece in (2, 3):
-            rim_copy(piece).wait_send()
+        rim_whole(False).wait_send()
 
     def own(low, high):
         def body(k, acc):
@@ -496,8 +502,8 @@
 
     cut = n_own // 2
     own(0, cut)
-    for k, part in enumerate((soon, (1, 2))):
-        arrive(second.at[0], turned + k)
+    arrive(second, turned)
+    for part in (soon, (1, 2)):
         for along in part:
             for slot in slots:
                 hand_on(slot, along)
@@ -526,9 +532,8 @@
         sums[row] += ext[help_order[3, row]] * help_order[4, row].astype(jnp.float32)
 
     late_table.wait()
-    for k in range(3):
-        link.whole(note_row(0), NOTES + k, 0, neighbour(0, 1)).wait_send()
-        link.whole(note_column(0), NOTES + 3 + k, 0, neighbour(0, 1)).wait_send()
+    link.whole(metas.at[0, pl.ds(0, 3)], NOTES, 0, neighbour(0, 1)).wait_send()
+    link.whole(metas.at[pl.ds(0, 3)], NOTES + 1, 0, neighbour(0, 1)).wait_send()
     arrive(second.at[0], ended + 3)
     acc = jnp.zeros(ext.shape[1:], jnp.float32)
     for at in range(2 * LATE):
@@ -577,10 +582,10 @@
             pltpu.SMEM((8, 256), i32),
             pltpu.SMEM((8, 256), i32),
             pltpu.SMEM((SIDE, SIDE, 3, 1, helps), i32),
-            pltpu.SemaphoreType.DMA((8,)),
-            pltpu.SemaphoreType.DMA((29,)),
             pltpu.SemaphoreType.DMA((4,)),
-            pltpu.SemaphoreType.DMA((4,)),
+            pltpu.SemaphoreType.DMA((28,)),
+            pltpu.SemaphoreType.DMA((2,)),
+            pltpu.SemaphoreType.DMA((2,)),
             pltpu.SemaphoreType.DMA((8,)),
             pltpu.SemaphoreType.DMA((2,)),
         ],

time: 117 us -> 117 us (level)
  no operation moved by 1% of the time
where the time goes in v6:
time: 117 us; the launch traced here: 116 us
  Pallas kernels  115 us (98%)
    pallas_call x1, Pallas kernels, local(): pl.pallas_call(exchange, out_shape=pltpu.VMEM(sims.shape, f32), in_specs=...  115 us

profile of v6, /device:TPU:1, one launch (start us, length us, event | category | flops | bytes accessed | tf_op | source)
XLA Modules:
  0.0 116.2 jit_solution(7491560725973034003)
XLA Ops:
  0.0 115.2 %exchange.1 = f32[16,128,128]{2,1,0:T(8,128)S(1)} custom-call(f32[16,128,128]{2,1,0:T(8,128)} %sims.1, f32[4,4,2,128,128]{4,3,2,1,0:T(8,128)} %bitcast.6, f32[192,128,128]{2,1,0:T(8,128)} %tiles.1, s32[1,192]{1,0:T(1,128)} %bitcast.7, s32[1,192]{1,0:T(1,128)} %bitcast.8, s32[1,32]{1,0:T(1,128)} %bitcast.9, s32[1,32]{1,0:T(1,128)} %bitcast.10, s32[1,32]{1,0:T(1,128)} %bitcast.11), custom_call_target="tpu_custom_call" | custom-call | tf_op jit(solution)/shard_map/exchange/pallas_call | solution.py:562
  115.3 1.0 copy.10

commit v7 on v6

--- a/solution.py
+++ b/solution.py
@@ -509,7 +509,7 @@
                 hand_on(slot, along)
     own(cut, n_own)
 
-    @pl.loop(0, blocks)
+    @pl.loop(0, blocks, unroll=4)
     def _(row):
         sums[row] = ext[order[3, row]] * order[4, row].astype(jnp.float32)
 
@@ -527,7 +527,7 @@
         acc = acc * keep + terms[help_order[0, at]] * live
         ext[at] = acc
 
-    @pl.loop(0, blocks)
+    @pl.loop(0, blocks, unroll=4)
     def _(row):
         sums[row] += ext[help_order[3, row]] * help_order[4, row].astype(jnp.float32)
 
@@ -544,7 +544,7 @@
         acc = acc * keep + product(split(tile), ext_parts[jnp.right_shift(load, 1)]) * live
         ext[at] = acc
 
-    @pl.loop(0, blocks)
+    @pl.loop(0, blocks, unroll=4)
     def _(row):
         sums_out[row] = sums[row] + ext[late_order[3, row]] * late_order[4, row].astype(jnp.float32)
 

time: 117 us -> 117 us (level)
  no operation moved by 1% of the time
where the time goes in v7:
time: 117 us; the launch traced here: 116 us
  Pallas kernels  115 us (98%)
    pallas_call x1, Pallas kernels, local(): pl.pallas_call(exchange, out_shape=pltpu.VMEM(sims.shape, f32), in_specs=...  115 us

profile of v7, /device:TPU:1, one launch (start us, length us, event | category | flops | bytes accessed | tf_op | source)
XLA Modules:
  0.0 116.1 jit_solution(7470525640499976281)
XLA Ops:
  0.0 115.2 %exchange.1 = f32[16,128,128]{2,1,0:T(8,128)S(1)} custom-call(f32[16,128,128]{2,1,0:T(8,128)} %sims.1, f32[4,4,2,128,128]{4,3,2,1,0:T(8,128)} %bitcast.6, f32[192,128,128]{2,1,0:T(8,128)} %tiles.1, s32[1,192]{1,0:T(1,128)} %bitcast.7, s32[1,192]{1,0:T(1,128)} %bitcast.8, s32[1,32]{1,0:T(1,128)} %bitcast.9, s32[1,32]{1,0:T(1,128)} %bitcast.10, s32[1,32]{1,0:T(1,128)} %bitcast.11), custom_call_target="tpu_custom_call" | custom-call | tf_op jit(solution)/shard_map/exchange/pallas_call | solution.py:562
  115.2 1.0 copy.10
